TPU v7x, 128 devices: a whole 4x4x4 slice. The times are simulated.
128 devices in a mesh: lat: 16 (over x, y), lon: 8 (over z, core).
Axes of the slice: x: 4, y: 4, z: 4, core: 2. Of those that a mesh axis runs over, the one named last changes fastest.
Arguments:
- state: float32 [3, 384, 49152], P(None, 'lat', 'lon'), may hold values from -6 to 6
- sigma: float32 [3, 384, 768], P(None, 'lat', 'lon'), may hold values from 0.3 to 3
- vert: float32 [3, 64, 64], replicated, may hold values from -0.75 to 0.75
- bal_temp: float32 [64, 64], replicated, may hold values from -0.75 to 0.75
- chi_coef: float32 [64], replicated, may hold values from -1 to 1
- scales: float32 [8], replicated, may hold values from 6 to 40
- classes: int32 [192], replicated, may hold values from 0 to 7
- owner: int32 [192], replicated, may hold values from 0 to 127, as said below
Outputs:
- applied: float32 [3, 384, 49152], P(None, 'lat', 'lon')
- slab_energy: float32 [128, 3], P(('lat', 'lon'))
Inputs may be any that keep to these rules, and one draw needn't show every extreme that they name: `owner`: every device owns at most 3 slabs, and some device owns exactly 3.
All inputs are finite; a program needn't handle non-finite values.
Results may differ from a plain program's by a relative error of at most 0.0003.
Values sent between devices are 32-bit elements; how exact they have to be, the bound alone decides.
A program may use at most 64 MiB of HBM per device.

v0:
```python
import jax
import jax.numpy as jnp
from jax import lax
from jax.sharding import PartitionSpec as P

highest = lax.Precision.HIGHEST


def with_halo(x, sides, width):
    for axis, dim in sides:
        devices, length = (lax.axis_size(axis), x.shape[dim])
        up = [(i, (i + 1) % devices) for i in range(devices - 1)]
        down = [(j, i) for i, j in up]
        last = lax.slice_in_dim(x, length - width, length, axis=dim)
        leading = lax.slice_in_dim(x, 0, width, axis=dim)
        before = lax.ppermute(last, axis, up)
        after = lax.ppermute(leading, axis, down)
        x = jnp.concatenate([before, x, after], axis=dim)
    return x


def laplace_tile(field):
    padded = with_halo(field, (("lat", 1), ("lon", 2)), 1)
    return (
        4.0 * field
        - padded[:, 2:, 1:-1]
        - padded[:, :-2, 1:-1]
        - padded[:, 1:-1, 2:]
        - padded[:, 1:-1, :-2]
    )


def filter_tables(length):
    idx = jnp.arange(128, dtype=jnp.float32)
    gap = idx[:, None] - idx[None, :]
    decay = jnp.exp(-1.0 / length)
    powers = jnp.exp(-jnp.maximum(gap, 0.0)[None] / length[:, None, None])
    lower = jnp.where(gap[None] >= 0.0, (1.0 - decay)[:, None, None] * powers, 0.0)
    ramp = jnp.exp(-(idx[None, :] + 1.0) / length[:, None])
    span = jnp.exp(-128.0 / length)
    return (lower, ramp, span)


def recursion(field, tables, along_lat, backward):
    lower, ramp, span = tables
    edge_pos = 0 if backward else 127
    if along_lat:
        form = "ckbj,cbd->ckdj" if backward else "ckbj,cdb->ckdj"
        local = jnp.einsum(form, field, lower, precision=highest)
        edges = local[:, :, edge_pos, :]
        blocks = local.shape[1]
    else:
        form = "cjkb,cbd->cjkd" if backward else "cjkb,cdb->cjkd"
        local = jnp.einsum(form, field, lower, precision=highest)
        edges = local[:, :, :, edge_pos]
        blocks = local.shape[2]
    order = list(range(blocks))
    if backward:
        order = order[::-1]
    state = jnp.zeros_like(edges[:, 0, :] if along_lat else edges[:, :, 0])
    carries = [state] * blocks
    for block in order:
        carries[block] = state
        edge = edges[:, block, :] if along_lat else edges[:, :, block]
        state = edge + span[:, None] * state
    weights = ramp[:, ::-1] if backward else ramp
    if along_lat:
        carry = jnp.stack(carries, axis=1)
        return local + carry[:, :, None, :] * weights[:, None, :, None]
    carry = jnp.stack(carries, axis=2)
    return local + carry[:, :, :, None] * weights[:, None, None, :]


def smooth(slabs, tables, amp):
    count, rows, cols = slabs.shape
    field = slabs.reshape(count, rows, cols // 128, 128)
    field = recursion(field, tables, False, False)
    field = recursion(field, tables, False, True)
    field = field.reshape(count, rows // 128, 128, cols)
    field = recursion(field, tables, True, False)
    field = recursion(field, tables, True, True)
    return field.reshape(count, rows, cols) * amp[:, None, None]


def shards(state, sigma, vert, bal_temp, chi_coef, scales, classes, owner):
    n_lat = lax.axis_size("lat")
    n_lon = lax.axis_size("lon")
    devices = n_lat * n_lon
    nvars = state.shape[0]
    levels = vert.shape[1]
    tile_lat = state.shape[1]
    tile_lon = state.shape[2] // levels
    tile_cells = tile_lat * tile_lon
    count = nvars * levels
    capacity = (count + devices - 1) // devices + 1
    index = jnp.arange(count, dtype=jnp.int32)
    same = (owner[:, None] == owner[None, :]) & (index[None, :] < index[:, None])
    slot = jnp.sum(same.astype(jnp.int32), axis=1)
    target = owner * capacity + slot
    source_of = jnp.full((devices * capacity,), count, jnp.int32).at[target].set(index)
    field = state.reshape(nvars, tile_lat, tile_lon, levels).transpose(0, 3, 1, 2)
    folded = jnp.einsum("lk,lij->kij", bal_temp, field[2], precision=highest)
    adj_psi = field[0] + chi_coef[:, None, None] * field[1] + laplace_tile(folded)
    scaled = jnp.stack([adj_psi, field[1], field[2]]) * sigma[:, None]
    w = jnp.einsum("vkl,vkij->vlij", vert, scaled, precision=highest)
    rows_ext = jnp.concatenate(
        [w.reshape(count, tile_cells), jnp.zeros((1, tile_cells), jnp.float32)], axis=0
    )
    outgoing = jnp.take(rows_ext, source_of, axis=0)
    arrived = lax.all_to_all(
        outgoing.reshape(devices, capacity, tile_cells),
        ("lat", "lon"),
        split_axis=0,
        concat_axis=0,
        tiled=True,
    )
    whole = arrived.reshape(n_lat, n_lon, capacity, tile_lat, tile_lon)
    whole = whole.transpose(2, 0, 3, 1, 4).reshape(capacity, n_lat * tile_lat, n_lon * tile_lon)
    rank = lax.axis_index("lat") * n_lon + lax.axis_index("lon")
    mine = lax.dynamic_slice_in_dim(source_of, rank * capacity, capacity)
    picks = (mine[:, None] == index[None, :]).astype(jnp.int32)
    my_class = jnp.sum(picks * classes[None, :], axis=1)
    class_ids = jnp.arange(scales.shape[0], dtype=jnp.int32)
    length = jnp.sum(
        jnp.where(my_class[:, None] == class_ids[None, :], scales[None, :], 0.0), axis=1
    )
    tables = filter_tables(length)
    amp = length**0.75
    ctrl = smooth(whole, tables, amp)
    slab_energy = jnp.mean(ctrl * ctrl, axis=(1, 2))[None, :]
    back = smooth(ctrl, tables, amp)
    pieces = back.reshape(capacity, n_lat, tile_lat, n_lon, tile_lon).transpose(1, 3, 0, 2, 4)
    pieces = pieces.reshape(n_lat, n_lon, capacity, tile_cells)
    returned = lax.all_to_all(
        pieces.reshape(devices, capacity, tile_cells),
        ("lat", "lon"),
        split_axis=0,
        concat_axis=0,
        tiled=True,
    )
    tiles = jnp.take(returned.reshape(devices * capacity, tile_cells), target, axis=0)
    tiles = tiles.reshape(nvars, levels, tile_lat, tile_lon)
    z = jnp.einsum("vlk,vkij->vlij", vert, tiles, precision=highest) * sigma[:, None]
    out_chi = z[1] + chi_coef[:, None, None] * z[0]
    out_temp = z[2] + jnp.einsum("lk,kij->lij", bal_temp, laplace_tile(z[0]), precision=highest)
    mixed = jnp.stack([z[0], out_chi, out_temp])
    applied = mixed.transpose(0, 2, 3, 1).reshape(nvars, tile_lat, tile_lon * levels)
    return (applied, slab_energy)


def solution(mesh):
    return jax.shard_map(
        shards,
        mesh=mesh,
        in_specs=(P(None, "lat", "lon"), P(None, "lat", "lon"), P(), P(), P(), P(), P(), P()),
        out_specs=(P(None, "lat", "lon"), P(("lat", "lon"), None)),
        check_vma=False,
    )
```

profile of v0, /device:TPU:3, one launch (start us, length us, event | category | flops | bytes accessed | tf_op | source)
XLA Modules:
  0.0 377.0 jit_solution(7609366422352671029)
XLA Ops:
  0.6 3.9 %reshape.577 = f32[3,24,96,64]{3,2,1,0:T(8,128)} reshape(f32[3,24,6144]{2,1,0:T(8,128)} %param.8) | data formatting | bytes 3538944 | tf_op jit(solution)/shard_map/reshape | solution.py:101
  4.6 2.5 copy.94
  8.0 4.6 %collective-permute-start = (f32[64,1,96]{2,0,1:T(8,128)S(1)}, f32[64,1,96]{2,0,1:T(8,128)S(1)}, u32[]{:S(2)}, u32[]{:S(2)}) collective-permute-start(f32[64,1,96]{2,0,1:T(8,128)S(1)} %get-tuple-element.46), channel_id=1, source_target_pairs={{8,0},{16,8},{24,16},{32,24},{40,32},{48,40},{56,48},{64,56},{72,6... | collective-permute-start | bytes 73736 | tf_op jit(solution)/shard_map/ppermute | solution.py:17
  16.0 3.4 collective-permute-done.1
  22.4 4.0 %collective-permute-start.2 = (f32[64,26,1]{0,2,1:T(1,128)S(1)}, f32[64,26,1]{0,2,1:T(1,128)S(1)}, u32[]{:S(2)}, u32[]{:S(2)}) collective-permute-start(f32[64,26,1]{0,2,1:T(1,128)S(1)} %copy.96), channel_id=1, source_target_pairs={{1,0},{2,1},{3,2},{4,3},{5,4},{6,5},{7,6},{9,8},{10,9},{11,10},{12... | collective-permute-start | bytes 19976 | tf_op jit(solution)/shard_map/ppermute | solution.py:17
  27.9 3.6 collective-permute-start.3
  37.8 2.5 fusion.38
  45.2 3.6 gather_fusion
  48.8 6.3 %gather.13 = f32[128,3,2304]{2,1,0:T(4,128)} reshape(f32[384,2304]{1,0:T(8,128)} %gather_fusion) | data formatting | bytes 7077888 | tf_op jit(solution)/shard_map/jit(_take)/gather | solution.py:109
  55.1 5.6 %broadcast_select_fusion = f32[128,3,2304]{2,1,0:T(4,128)} fusion(f32[128,3,2304]{2,1,0:T(4,128)} %gather.13, pred[128,3]{1,0:T(8,128)(4,1)S(1)} %broadcast_in_dim.59), kind=kLoop, calls=%fused_computation.40 | loop fusion | flops 884736 | bytes 7078272 | tf_op jit(solution)/shard_map/jit(_take)/select_n | solution.py:109
  60.7 8.0 %all-to-all-start = ((f32[128,3,2304]{2,1,0:T(4,128)}), f32[128,3,2304]{2,1,0:T(4,128)}, u32[]{:S(2)}, u32[]{:S(2)}) async-start(f32[128,3,2304]{2,1,0:T(4,128)} %broadcast_select_fusion), calls=%async_computation | async-start | bytes 9437184 | tf_op jit(solution)/shard_map/all_to_all | solution.py:110
  69.6 56.1 %all-to-all-done = f32[128,3,2304]{2,1,0:T(4,128)} async-done(((f32[128,3,2304]{2,1,0:T(4,128)}), f32[128,3,2304]{2,1,0:T(4,128)}, u32[]{:S(2)}, u32[]{:S(2)}) %all-to-all-start) | async-done | bytes 3538976 | tf_op jit(solution)/shard_map/all_to_all | solution.py:110
  125.6 4.8 %copy.102 = f32[128,3,2304]{2,0,1:T(8,128)} copy(f32[128,3,2304]{2,1,0:T(4,128)} %all-to-all-done) | data formatting | bytes 7077888 | tf_op jit(solution)/shard_map/all_to_all | solution.py:110
  130.4 6.2 %reshape.579 = f32[16,8,3,24,96]{4,3,1,0,2:T(8,128)} reshape(f32[128,3,2304]{2,0,1:T(8,128)} %copy.102) | data formatting | bytes 7077888 | tf_op jit(solution)/shard_map/reshape | solution.py:117
  136.6 5.5 %copy.103 = f32[3,16,24,8,96]{4,3,2,1,0:T(8,128)} copy(f32[3,16,24,8,96]{4,2,3,1,0:T(8,128)} %bitcast.137) | data formatting | bytes 7077888 | tf_op jit(solution)/shard_map/transpose | solution.py:118
  142.1 6.6 %reshape_reshape.6 = f32[3,384,6,128]{3,2,1,0:T(8,128)} reshape(f32[3,16,24,8,96]{4,3,2,1,0:T(8,128)} %copy.103) | data formatting | bytes 7077888 | tf_op jit(solution)/shard_map/reshape;reshape | solution.py:76
  148.8 6.1 %fusion.6 = f32[3,384,6,128]{1,3,2,0:T(8,128)S(1)} fusion(f32[3,384,6,128]{3,2,1,0:T(8,128)} %reshape_reshape.6, f32[3]{0:T(128)S(1)} %select_reduce_fusion.1, f32[128,128]{0,1:T(8,128)S(1)} %maximum_negate_fusion, f32[3]{0:T(128)S(1)} %get-tuple-element.48, pred[128,128]{0,1:T(8,128)(4,1)S(1)} %fusion.121), kind=kOutput, calls=%fused_computation.15 | convolution fusion | flops 1359101952 | bytes 7159832 | tf_op jit(solution)/shard_map/cjkb,cdb->cjkd/dot_general | solution.py:54
  156.8 5.9 %fusion.17 = f32[3,384,6,128]{1,3,2,0:T(8,128)S(1)} fusion(f32[3,384,6,128]{1,3,2,0:T(8,128)} %copy-done.3, f32[3,128]{1,0:T(4,128)S(1)} %divide_exponential_fusion.1, f32[3,384,6]{1,2,0:T(8,128)S(1)} %stack.27, f32[3]{0:T(128)S(1)} %select_reduce_fusion.1, f32[128,128]{0,1:T(8,128)S(1)} %maximum_negate_fusion, f32[3]{0:T(128)S(1)} %get-tuple-element.48, ...), kind=kOutput, calls=%fused_computation.28 | convolution fusion | flops 1360871424 | bytes 7189016 | tf_op jit(solution)/shard_map/cjkb,cbd->cjkd/dot_general | solution.py:54
  164.7 4.2 %multiply_add_fusion.3 = f32[3,384,6,128]{1,3,2,0:T(8,128)} fusion(f32[3,384,6,128]{1,3,2,0:T(8,128)} %copy-done.2, f32[3,128]{1,0:T(4,128)S(1)} %rev.2, f32[3,384,6]{1,2,0:T(8,128)S(1)} %stack.28), kind=kLoop, calls=%fused_computation.27 | loop fusion | flops 1769472 | bytes 7107072 | tf_op jit(solution)/shard_map/add | solution.py:71
  168.8 6.7 %reshape.622 = f32[3,3,128,768]{2,1,3,0:T(4,128)} reshape(f32[3,384,6,128]{1,3,2,0:T(8,128)} %multiply_add_fusion.3) | data formatting | bytes 7077888 | tf_op jit(solution)/shard_map/reshape | solution.py:79
  175.5 5.8 %fusion.24 = f32[3,3,128,768]{3,2,1,0:T(8,128)S(1)} fusion(f32[3,3,128,768]{2,1,3,0:T(4,128)} %reshape.622, f32[3]{0:T(128)S(1)} %select_reduce_fusion.1, f32[128,128]{0,1:T(8,128)S(1)} %maximum_negate_fusion, f32[3]{0:T(128)S(1)} %get-tuple-element.48, pred[128,128]{0,1:T(8,128)(4,1)S(1)} %fusion.121), kind=kOutput, calls=%fused_computation.41 | convolution fusion | flops 1359101952 | bytes 7159832 | tf_op jit(solution)/shard_map/ckbj,cdb->ckdj/dot_general | solution.py:49
  181.5 3.4 fusion.14
  187.5 4.4 %multiply_reduce_fusion = (f32[3]{0:T(128)S(1)}, f32[3,3,128,768]{3,1,0,2:T(4,128)S(1)}) fusion(f32[3]{0:T(128)S(1)} %get-tuple-element.47, f32[3,128]{0,1:T(8,128)S(1)} %copy.112, f32[3,3,768]{2,1,0:T(4,128)S(1)} %pad_maximum_fusion.25, f32[3,128,3,768]{3,1,2,0:T(8,128)S(1)} %fusion.14), kind=kLoop, calls=%fused_computation.5 | loop fusion | flops 4423677 | bytes 7107096 | tf_op jit(solution)/shard_map/reduce_sum | solution.py:130
  194.3 4.8 %reshape.581 = f32[3,384,6,128]{3,2,1,0:T(8,128)} reshape(f32[3,3,128,768]{3,2,1,0:T(8,128)} %copy.113) | data formatting | bytes 7077888 | tf_op jit(solution)/shard_map/reshape | solution.py:82
  199.1 2.7 broadcast_multiply_fusion
  201.8 3.7 fusion.4
  207.5 5.9 %fusion.11 = f32[3,384,6,128]{1,3,2,0:T(8,128)S(1)} fusion(f32[3,384,6,128]{1,3,2,0:T(8,128)} %copy-done.4, f32[3,384,6]{1,2,0:T(8,128)S(1)} %stack.31, f32[3,128]{1,0:T(4,128)S(1)} %divide_exponential_fusion.1, f32[3]{0:T(128)S(1)} %select_reduce_fusion.1, f32[128,128]{0,1:T(8,128)S(1)} %maximum_negate_fusion, f32[3]{0:T(128)S(1)} %get-tuple-element.48, ...), kind=kOutput, calls=%fused_computation.21 | convolution fusion | flops 1360871424 | bytes 7189016 | tf_op jit(solution)/shard_map/cjkb,cbd->cjkd/dot_general | solution.py:54
  215.4 4.2 %multiply_add_fusion.2 = f32[3,384,6,128]{1,3,2,0:T(8,128)} fusion(f32[3,384,6,128]{1,3,2,0:T(8,128)} %copy-done.1, f32[3,384,6]{1,2,0:T(8,128)S(1)} %stack.32, f32[3,128]{1,0:T(4,128)S(1)} %rev.2), kind=kLoop, calls=%fused_computation.20 | loop fusion | flops 1769472 | bytes 7107072 | tf_op jit(solution)/shard_map/add | solution.py:71
  219.6 6.5 %reshape.623 = f32[3,3,128,768]{2,1,3,0:T(4,128)} reshape(f32[3,384,6,128]{1,3,2,0:T(8,128)} %multiply_add_fusion.2) | data formatting | bytes 7077888 | tf_op jit(solution)/shard_map/reshape | solution.py:79
  226.1 5.8 %fusion.27 = f32[3,3,128,768]{3,2,1,0:T(8,128)S(1)} fusion(f32[3,3,128,768]{2,1,3,0:T(4,128)} %reshape.623, f32[3]{0:T(128)S(1)} %select_reduce_fusion.1, f32[128,128]{0,1:T(8,128)S(1)} %maximum_negate_fusion, f32[3]{0:T(128)S(1)} %get-tuple-element.48, pred[128,128]{0,1:T(8,128)(4,1)S(1)} %fusion.121), kind=kOutput, calls=%fused_computation.42 | convolution fusion | flops 1359101952 | bytes 7159832 | tf_op jit(solution)/shard_map/ckbj,cdb->ckdj/dot_general | solution.py:49
  232.1 3.4 fusion.8
  238.0 3.1 multiply_add_fusion
  243.6 5.9 %reshape.583 = f32[3,16,24,8,96]{4,3,2,1,0:T(8,128)} reshape(f32[3,3,128,768]{3,2,1,0:T(8,128)} %copy.122) | data formatting | bytes 7077888 | tf_op jit(solution)/shard_map/reshape | solution.py:82
  249.4 3.1 multiply_bitcast_fusion
  252.6 3.0 copy.154
  255.5 7.9 %reshape.624 = f32[128,3,2304]{2,1,0:T(4,128)} reshape(f32[16,8,3,24,96]{4,3,2,1,0:T(8,128)} %copy.154) | data formatting | bytes 7077888 | tf_op jit(solution)/shard_map/reshape;reshape | solution.py:135
  263.5 7.7 %all-to-all-start.1 = ((f32[128,3,2304]{2,1,0:T(4,128)}), f32[128,3,2304]{2,1,0:T(4,128)}, u32[]{:S(2)}, u32[]{:S(2)}) async-start(f32[128,3,2304]{2,1,0:T(4,128)} %reshape.624), calls=%async_computation.1 | async-start | bytes 9437184 | tf_op jit(solution)/shard_map/all_to_all | solution.py:134
  271.2 57.0 %all-to-all-done.1 = f32[128,3,2304]{2,1,0:T(4,128)} async-done(((f32[128,3,2304]{2,1,0:T(4,128)}), f32[128,3,2304]{2,1,0:T(4,128)}, u32[]{:S(2)}, u32[]{:S(2)}) %all-to-all-start.1) | async-done | bytes 3538976 | tf_op jit(solution)/shard_map/all_to_all | solution.py:134
  328.3 6.5 %reshape.584 = f32[384,2304]{1,0:T(8,128)} reshape(f32[128,3,2304]{2,1,0:T(4,128)} %all-to-all-done.1) | data formatting | bytes 7077888 | tf_op jit(solution)/shard_map/reshape | solution.py:141
  334.8 5.2 %gather_fusion.1 = f32[192,2304]{1,0:T(8,128)} fusion(f32[384,2304]{1,0:T(8,128)} %reshape.584, s32[1024]{0:T(1024)S(1)} %pad_clamp_fusion), kind=kCustom, calls=%fused_computation.1 | custom fusion | bytes 3539712 | tf_op jit(solution)/shard_map/jit(_take)/gather | solution.py:141
  340.0 2.9 gather.15
  342.9 2.6 multiply_bitcast_fusion.1
  346.9 3.4 collective-permute-start.4
  352.3 4.8 %collective-permute-done.5 = f32[64,1,96]{2,0,1:T(8,128)S(1)} collective-permute-done((f32[64,1,96]{2,0,1:T(8,128)S(1)}, f32[64,1,96]{2,0,1:T(8,128)S(1)}, u32[]{:S(2)}, u32[]{:S(2)}) %collective-permute-start.5) | collective-permute-done | bytes 24608 | tf_op jit(solution)/shard_map/ppermute | solution.py:16
  357.8 4.5 %collective-permute-start.6 = (f32[64,26,1]{0,2,1:T(1,128)S(1)}, f32[64,26,1]{0,2,1:T(1,128)S(1)}, u32[]{:S(2)}, u32[]{:S(2)}) collective-permute-start(f32[64,26,1]{0,2,1:T(1,128)S(1)} %copy.126), channel_id=1, source_target_pairs={{1,0},{2,1},{3,2},{4,3},{5,4},{6,5},{7,6},{9,8},{10,9},{11,10},{12... | collective-permute-start | bytes 19976 | tf_op jit(solution)/shard_map/ppermute | solution.py:17
  366.1 2.5 fusion.40
  370.0 2.5 copy.130
  372.5 4.0 %reshape.585 = f32[3,24,6144]{2,1,0:T(8,128)} reshape(f32[3,24,96,64]{3,2,1,0:T(8,128)} %copy.130) | data formatting | bytes 3538944 | tf_op jit(solution)/shard_map/reshape | solution.py:147
  (114 shorter events, 47.7 us)
Async XLA Ops:
  0.6 37.1 %copy-start = (f32[3,64,64]{2,1,0:T(8,128)S(1)}, f32[3,64,64]{2,1,0:T(8,128)}, u32[]{:S(2)}) copy-start(f32[3,64,64]{2,1,0:T(8,128)} %param.10) | copy-start | bytes 147460
  4.5 2.6 copy-start.8
  4.5 10.0 %copy-start.9 = (s32[192]{0:T(256)S(1)}, s32[192]{0:T(256)}, u32[]{:S(2)}) copy-start(s32[192]{0:T(256)} %param.15) | copy-start | bytes 2308
  8.0 8.0 %collective-permute-start = (f32[64,1,96]{2,0,1:T(8,128)S(1)}, f32[64,1,96]{2,0,1:T(8,128)S(1)}, u32[]{:S(2)}, u32[]{:S(2)}) collective-permute-start(f32[64,1,96]{2,0,1:T(8,128)S(1)} %get-tuple-element.46), channel_id=1, source_target_pairs={{8,0},{16,8},{24,16},{32,24},{40,32},{48,40},{56,48},{64,56},{72,6... | collective-permute-start | bytes 73736 | tf_op jit(solution)/shard_map/ppermute | solution.py:17
  12.6 6.8 %collective-permute-start.1 = (f32[64,1,96]{2,0,1:T(8,128)S(1)}, f32[64,1,96]{2,0,1:T(8,128)S(1)}, u32[]{:S(2)}, u32[]{:S(2)}) collective-permute-start(f32[64,1,96]{2,0,1:T(8,128)S(1)} %get-tuple-element.45), channel_id=1, source_target_pairs={{0,8},{8,16},{16,24},{24,32},{32,40},{40,48},{48,56},{56,64},{64,7... | collective-permute-start | bytes 73736 | tf_op jit(solution)/shard_map/ppermute | solution.py:16
  20.9 14.7 %copy-start.10 = (f32[64]{0:T(128)S(1)}, f32[64]{0:T(128)}, u32[]{:S(2)}) copy-start(f32[64]{0:T(128)} %param.12) | copy-start | bytes 772
  22.4 10.6 %collective-permute-start.2 = (f32[64,26,1]{0,2,1:T(1,128)S(1)}, f32[64,26,1]{0,2,1:T(1,128)S(1)}, u32[]{:S(2)}, u32[]{:S(2)}) collective-permute-start(f32[64,26,1]{0,2,1:T(1,128)S(1)} %copy.96), channel_id=1, source_target_pairs={{1,0},{2,1},{3,2},{4,3},{5,4},{6,5},{7,6},{9,8},{10,9},{11,10},{12... | collective-permute-start | bytes 19976 | tf_op jit(solution)/shard_map/ppermute | solution.py:17
  27.9 6.4 %collective-permute-start.3 = (f32[64,26,1]{0,2,1:T(1,128)S(1)}, f32[64,26,1]{0,2,1:T(1,128)S(1)}, u32[]{:S(2)}, u32[]{:S(2)}) collective-permute-start(f32[64,26,1]{0,2,1:T(1,128)S(1)} %copy.98), channel_id=1, source_target_pairs={{0,1},{1,2},{2,3},{3,4},{4,5},{5,6},{6,7},{8,9},{9,10},{10,11},{11... | collective-permute-start | bytes 19976 | tf_op jit(solution)/shard_map/ppermute | solution.py:16
  32.8 5.0 %copy-start.7 = (f32[3,24,96]{2,1,0:T(8,128)S(1)}, f32[3,24,96]{2,1,0:T(8,128)}, u32[]{:S(2)}) copy-start(f32[3,24,96]{2,1,0:T(8,128)} %param.9) | copy-start | bytes 82948
  35.6 2.2 copy-start.6
  60.7 8.1 %copy-start.11 = (s32[192]{0:T(256)S(1)}, s32[192]{0:T(256)}, u32[]{:S(2)}) copy-start(s32[192]{0:T(256)} %param.14) | copy-start | bytes 2308
  60.7 8.3 %copy-start.12 = (f32[8]{0:T(128)S(1)}, f32[8]{0:T(128)}, u32[]{:S(2)}) copy-start(f32[8]{0:T(128)} %param.13) | copy-start | bytes 100
  60.7 64.9 %all-to-all-start = ((f32[128,3,2304]{2,1,0:T(4,128)}), f32[128,3,2304]{2,1,0:T(4,128)}, u32[]{:S(2)}, u32[]{:S(2)}) async-start(f32[128,3,2304]{2,1,0:T(4,128)} %broadcast_select_fusion), calls=%async_computation | async-start | bytes 9437184 | tf_op jit(solution)/shard_map/all_to_all | solution.py:110
  154.9 1.7 copy-start.3
  162.7 1.7 copy-start.2
  205.6 1.7 copy-start.4
  213.4 1.7 copy-start.1
  263.5 64.8 %all-to-all-start.1 = ((f32[128,3,2304]{2,1,0:T(4,128)}), f32[128,3,2304]{2,1,0:T(4,128)}, u32[]{:S(2)}, u32[]{:S(2)}) async-start(f32[128,3,2304]{2,1,0:T(4,128)} %reshape.624), calls=%async_computation.1 | async-start | bytes 9437184 | tf_op jit(solution)/shard_map/all_to_all | solution.py:134
  345.5 12.0 %copy-start.5 = (f32[3,64,24,96]{3,1,2,0:T(8,128)}, f32[3,64,24,96]{3,1,2,0:T(8,128)S(1)}, u32[]{:S(2)}) copy-start(f32[3,64,24,96]{3,1,2,0:T(8,128)S(1)} %multiply_bitcast_fusion.1) | copy-start | bytes 5308420
  346.9 5.3 %collective-permute-start.4 = (f32[64,1,96]{2,0,1:T(8,128)S(1)}, f32[64,1,96]{2,0,1:T(8,128)S(1)}, u32[]{:S(2)}, u32[]{:S(2)}) collective-permute-start(f32[64,1,96]{2,0,1:T(8,128)S(1)} %get-tuple-element.44), channel_id=1, source_target_pairs={{8,0},{16,8},{24,16},{32,24},{40,32},{48,40},{56,48},{64,56},{72,6... | collective-permute-start | bytes 73736 | tf_op jit(solution)/shard_map/ppermute | solution.py:17
  350.3 6.8 %collective-permute-start.5 = (f32[64,1,96]{2,0,1:T(8,128)S(1)}, f32[64,1,96]{2,0,1:T(8,128)S(1)}, u32[]{:S(2)}, u32[]{:S(2)}) collective-permute-start(f32[64,1,96]{2,0,1:T(8,128)S(1)} %get-tuple-element.43), channel_id=1, source_target_pairs={{0,8},{8,16},{16,24},{24,32},{32,40},{40,48},{48,56},{56,64},{64,7... | collective-permute-start | bytes 73736 | tf_op jit(solution)/shard_map/ppermute | solution.py:16
  357.8 7.6 %collective-permute-start.6 = (f32[64,26,1]{0,2,1:T(1,128)S(1)}, f32[64,26,1]{0,2,1:T(1,128)S(1)}, u32[]{:S(2)}, u32[]{:S(2)}) collective-permute-start(f32[64,26,1]{0,2,1:T(1,128)S(1)} %copy.126), channel_id=1, source_target_pairs={{1,0},{2,1},{3,2},{4,3},{5,4},{6,5},{7,6},{9,8},{10,9},{11,10},{12... | collective-permute-start | bytes 19976 | tf_op jit(solution)/shard_map/ppermute | solution.py:17
  362.6 3.1 collective-permute-start.7
where the time goes:
time: 383 us; the launch traced here: 377 us
  local copies, waits for them, and re-layouts  129 us (34%)
  waiting for transfers between devices  121 us (32%)
  matrix products  48.5 us (13%)
  starting transfers between devices  41.9 us (11%)
  other arithmetic  34.6 us (9%)
    all_to_all x1, waiting for transfers between devices, shards(): lax.all_to_all(pieces.reshape(devices, capacity, tile_cells), ('lat', 'lo...  57 us
    all_to_all x1, waiting for transfers between devices, shards(): lax.all_to_all(outgoing.reshape(devices, capacity, tile_cells), ('lat', '...  56.1 us
    dot_general x8, matrix products, recursion(): local = jnp.einsum(form, field, lower, precision=highest)  40 us
    ppermute x4, starting transfers between devices, with_halo(): after = lax.ppermute(leading, axis, down)  16.6 us
    reshape x2, local copies, waits for them, and re-layouts, smooth(): field = field.reshape(count, rows // 128, 128, cols)  13.2 us
    another operation x2, local copies, waits for them, and re-layouts, shards(): pieces.reshape(devices, capacity, tile_cells)  10.9 us
    reshape x2, local copies, waits for them, and re-layouts, smooth(): return field.reshape(count, rows, cols) * amp[:, None, None]  10.7 us
    gather x2, local copies, waits for them, and re-layouts, shards(): outgoing = jnp.take(rows_ext, source_of, axis=0)  9.89 us
  transfers between devices with their start and end apart: 10, of which 4 were waited for; matrix products, arithmetic and copies ran while one was open for 2% of the time, Pallas kernels for 0%

commit v1 on v0

v1 whole, which is shorter than its diff:
```python
import functools

import jax
import jax.numpy as jnp
from jax import lax
from jax.experimental import pallas as pl
from jax.experimental.pallas import tpu as pltpu
from jax.sharding import PartitionSpec as P

F32 = jnp.float32
BF16 = jnp.bfloat16
MESH = pl.DeviceIdType.MESH


def split_product(x, w):
    hi = x.astype(BF16)
    lo = (x - hi.astype(F32)).astype(BF16)
    y = jnp.dot(jnp.concatenate([hi, lo], axis=1), w, preferred_element_type=F32)
    return y[:, :128] + y[:, 128:]


def swap(x):
    return pltpu.roll(x, 64, 1)


def rows_of(parts):
    return jnp.concatenate(parts, axis=0)


def kernel(
    dims,
    state_ref,
    sigma_ref,
    vert_ref,
    bal_ref,
    small_ref,
    out_ref,
    energy_ref,
    mats,
    pad,
    sig,
    temp,
    w,
    xs,
    xu,
    yf,
    ys,
    yu,
    xtab,
    ytab,
    edge_rows,
    halo_send,
    halo_recv,
    x_send,
    x_recv,
    x_back,
    x_home,
    y_send,
    y_recv,
    y_back,
    y_home,
    e_send,
    e_recv,
    f_send,
    f_recv,
    halo_ss,
    halo_rs,
    x_ss,
    x_rs,
    xb_ss,
    xb_rs,
    y_ss,
    y_rs,
    yb_ss,
    yb_rs,
    e_ss,
    e_rs,
    f_ss,
    f_rs,
):
    n_lat, n_lon, rows, cols = dims
    half = cols // 2
    jj_n = half // n_lat
    y_rows = 3 * jj_n * 4 + 4
    x_rows = 24
    v_base = (0, half + 8, 2 * half + 8)
    y_stride = 3 * half + 8
    la = lax.axis_index("lat")
    lo = lax.axis_index("lon")

    barrier = pltpu.get_barrier_semaphore()
    for o in range(1, n_lat):
        pl.semaphore_signal(barrier, inc=1, device_id=(lax.rem(la + o, n_lat), lo), device_id_type=MESH)
    for o in range(1, n_lon):
        pl.semaphore_signal(barrier, inc=1, device_id=(la, lax.rem(lo + o, n_lon)), device_id_type=MESH)

    lane = lax.broadcasted_iota(jnp.int32, (8, 128), 1)
    low1 = lane[:1] < 64

    def low(x):
        return jnp.broadcast_to(low1, x.shape)

    def pick(a, b):
        return jnp.where(low(a), a, b)

    small = small_ref[...]
    length = [small[v : v + 1] for v in range(3)]
    coupling = small[3:4]
    decay = [jnp.exp(-1.0 / r) for r in length]

    def power(v, k):
        return jnp.exp(-float(k) / length[v])

    def through(v, n):
        a = decay[v]
        return float(n) * power(v, n), a * (1.0 - power(v, 2 * n)) / (1.0 - a * a)

    def fill_table(ref, n):
        pos = lax.broadcasted_iota(jnp.int32, (n, 128), 0).astype(F32)
        for v in range(3):
            a, r = decay[v], length[v]
            first = jnp.exp(-(pos + 1.0) / r)
            tail = 1.0 - jnp.exp(-2.0 * (n - 1.0 - pos) / r)
            second = (pos + 1.0) * first + first * (a * a) * tail / (1.0 - a * a)
            ref[pl.ds(v * n, n), :] = first
            ref[pl.ds((3 + v) * n, n), :] = second

    fill_table(xtab, half)
    fill_table(ytab, rows)

    gain = []
    for v in range(3):
        a = decay[v]
        c = (1.0 - a) / (1.0 + a)
        gain.append(length[v] * jnp.sqrt(length[v]) * (c * c) * (c * c))

    def put_matrix(slot, m):
        pad[:, :64] = m
        top = pad[...]
        full = rows_of([top, swap(top)])
        hi = full.astype(BF16)
        low_part = (full - hi.astype(F32)).astype(BF16)
        mats[slot] = rows_of(
            [
                jnp.concatenate([hi, low_part], axis=1),
                jnp.concatenate([hi, jnp.zeros_like(hi)], axis=1),
            ]
        )

    pad[...] = jnp.zeros_like(pad)
    for v in range(3):
        put_matrix(v, vert_ref[v])
        put_matrix(3 + v, (vert_ref[v] * gain[v][:, :64]).T)
    put_matrix(6, bal_ref[...])
    put_matrix(7, bal_ref[...].T)

    for v in range(3):
        sig[pl.ds(v * rows, rows), :] = jnp.zeros((rows, 128), F32)
        sig[pl.ds(v * rows, rows), :cols] = sigma_ref[v]
    column = jnp.where(lax.broadcasted_iota(jnp.int32, (rows, 128), 1) < 64, 0, half)

    def spread(tile, j):
        return jnp.take_along_axis(tile, column + j, axis=1, mode="promise_in_bounds")

    def block(ref, at):
        return ref[pl.ds(pl.multiple_of(at, 8), rows), :]

    def put_block(ref, at, value):
        ref[pl.ds(pl.multiple_of(at, 8), rows), :] = value

    def pair(k, _):
        for v in range(3):
            n1 = state_ref[v, :, pl.ds(pl.multiple_of(k * 128, 128), 128)]
            n2 = state_ref[v, :, pl.ds(pl.multiple_of((k + half // 2) * 128, 128), 128)]
            even = pick(n1, swap(n2))
            odd = pick(swap(n1), n2)
            if v == 2:
                put_block(temp, (2 * k + 1) * rows, even)
                put_block(temp, (2 * k + 2) * rows, odd)
            else:
                put_block(w, (2 * k * 3 + v) * rows, even)
                put_block(w, ((2 * k + 1) * 3 + v) * rows, odd)
        return 0

    lax.fori_loop(0, half // 2, pair, 0)

    sig0 = sig[pl.ds(0, rows), :]
    msg_r, msg_c = half + rows, 2 * rows
    halo_send[pl.ds(0, half), :] = temp[pl.ds(rows, half, stride=rows), :]
    halo_send[pl.ds(half, rows), :] = sig0
    halo_send[pl.ds(msg_r, half), :] = temp[pl.ds(2 * rows - 1, half, stride=rows), :]
    halo_send[pl.ds(msg_r + half, rows), :] = sig0
    halo_send[pl.ds(2 * msg_r, rows), :] = temp[pl.ds(rows, rows), :]
    halo_send[pl.ds(2 * msg_r + rows, rows), :] = sig0
    halo_send[pl.ds(2 * msg_r + msg_c, rows), :] = temp[pl.ds(half * rows, rows), :]
    halo_send[pl.ds(2 * msg_r + msg_c + rows, rows), :] = sig0

    pl.semaphore_wait(barrier, n_lat + n_lon - 2)

    up = (lax.rem(la + n_lat - 1, n_lat), lo)
    down = (lax.rem(la + 1, n_lat), lo)
    left = (la, lax.rem(lo + n_lon - 1, n_lon))
    right = (la, lax.rem(lo + 1, n_lon))
    starts = (0, msg_r, 2 * msg_r, 2 * msg_r + msg_c)
    sizes = (msg_r, msg_r, msg_c, msg_c)
    halo = []
    for q, device in enumerate((up, down, left, right)):
        here = pl.ds(starts[q], sizes[q])
        copy = pltpu.make_async_remote_copy(
            src_ref=halo_send.at[here],
            dst_ref=halo_recv.at[here],
            send_sem=halo_ss.at[q],
            recv_sem=halo_rs.at[q],
            device_id=device,
            device_id_type=MESH,
        )
        copy.start()
        halo.append(copy)

    def batch(b):
        return [b * 8 + t for t in range(8)]

    def mix_in(b, _):
        js = batch(b)
        chi = [block(w, (j * 3 + 1) * rows) for j in js]
        for t, j in enumerate(js):
            at = j * 3 * rows
            put_block(w, at, block(w, at) + coupling * chi[t])
        for v, parts in ((1, chi), (2, [block(temp, (j + 1) * rows) for j in js])):
            y = split_product(rows_of(parts), mats[v])
            tile = sig[pl.ds(v * rows, rows), :]
            for t, j in enumerate(js):
                put_block(w, (j * 3 + v) * rows, y[t * rows : (t + 1) * rows] * spread(tile, j))
        return 0

    lax.fori_loop(0, half // 8, mix_in, 0)

    for copy in halo:
        copy.wait()
    has_up = jnp.where(la > 0, 1.0, 0.0).astype(F32)
    has_down = jnp.where(la < n_lat - 1, 1.0, 0.0).astype(F32)
    has_left = jnp.where(lo > 0, 1.0, 0.0).astype(F32)
    has_right = jnp.where(lo < n_lon - 1, 1.0, 0.0).astype(F32)
    edge_rows[pl.ds(0, half), :] = halo_recv[pl.ds(msg_r, half), :] * has_up
    edge_rows[pl.ds(half, half), :] = halo_recv[pl.ds(0, half), :] * has_down
    from_right = halo_recv[pl.ds(2 * msg_r, rows), :] * has_right
    from_left = halo_recv[pl.ds(2 * msg_r + msg_c, rows), :] * has_left

    def close_columns(lo_edge, hi_edge):
        put_block(temp, 0, pick(lo_edge, swap(temp[pl.ds(half * rows, rows), :])))
        put_block(temp, (half + 1) * rows, pick(swap(temp[pl.ds(rows, rows), :]), hi_edge))

    close_columns(swap(from_left), swap(from_right))
    row_id = lax.broadcasted_iota(jnp.int32, (rows, 128), 0)

    def laplace(j):
        x = block(temp, (j + 1) * rows)
        above = jnp.where(row_id == 0, edge_rows[pl.ds(j, 1), :], pltpu.roll(x, 1, 0))
        below = jnp.where(row_id == rows - 1, edge_rows[pl.ds(half + j, 1), :], pltpu.roll(x, rows - 1, 0))
        return 4.0 * x - above - below - block(temp, j * rows) - block(temp, (j + 2) * rows)

    def mix_psi(b, _):
        js = batch(b)
        y = split_product(rows_of([laplace(j) for j in js]), mats[6])
        y = y + rows_of([block(w, j * 3 * rows) for j in js])
        y = split_product(y, mats[0])
        for t, j in enumerate(js):
            put_block(w, j * 3 * rows, y[t * rows : (t + 1) * rows] * spread(sig0, j))
        return 0

    lax.fori_loop(0, half // 8, mix_psi, 0)

    def tall(per_v):
        return rows_of([jnp.broadcast_to(c, (rows, 128)) for c in per_v])

    ax = tall(decay)
    full = 3 * rows
    zero_x = jnp.zeros((full, 128), F32)

    def line(ref, j):
        return ref[pl.ds(pl.multiple_of(j * full, 8), full), :]

    def put_line(ref, j, value):
        ref[pl.ds(pl.multiple_of(j * full, 8), full), :] = value

    def x_forward(src):
        def step(j, s):
            s = ax * s + line(src, j)
            put_line(xs, j, s)
            return s

        return lax.fori_loop(0, half, step, zero_x, unroll=4)

    def x_backward(src, dst):
        def step(q, t):
            j = half - 1 - q
            t = ax * t
            put_line(dst, j, line(xs, j) + t)
            return line(src, j) + t

        return lax.fori_loop(0, half, step, zero_x, unroll=4)

    s1 = x_forward(w)
    t1 = x_backward(w, xu)
    s2 = x_forward(xu)
    t2 = x_backward(xu, xs)

    ah = tall([power(v, half) for v in range(3)])
    g1 = tall([through(v, half)[0] for v in range(3)])
    g2 = tall([through(v, half)[1] for v in range(3)])
    s1r, t1r, s2r, t2r = swap(s1), swap(t1), swap(s2), swap(t2)
    q0 = pick(ah * s1 + s1r, s2 + g1 * s1r + ah * (s2r + g2 * t1))
    q1 = pick(t1 + ah * t1r, t2r + g1 * t1 + ah * (t2 + g2 * s1r))
    groups = rows // 8

    for i, q in enumerate((q0, q1)):
        for v in range(3):
            for g in range(groups):
                at = v * rows + g * 8
                x_send[pl.ds((v * groups + g) * 2 + i, 8, stride=x_rows), :] = q[at : at + 8]

    def exchange(axis, me, n, size, src, dst, ss, rs):
        copies = []
        for o in range(1, n):
            other = lax.rem(me + o, n)
            device = (other, lo) if axis == "lat" else (la, other)
            copy = pltpu.make_async_remote_copy(
                src_ref=src.at[pl.ds(pl.multiple_of(other * size, 8), size)],
                dst_ref=dst.at[pl.ds(pl.multiple_of(me * size, 8), size)],
                send_sem=ss.at[other],
                recv_sem=rs.at[me],
                device_id=device,
                device_id_type=MESH,
            )
            copy.start()
            copies.append(copy)
        mine = pl.ds(pl.multiple_of(me * size, 8), size)
        dst[mine, :] = src[mine, :]
        return copies

    def arrive(axis, me, n, size, src, dst, ss, rs):
        for o in range(1, n):
            other = lax.rem(me + o, n)
            device = (other, lo) if axis == "lat" else (la, other)
            pltpu.make_async_remote_copy(
                src_ref=src.at[pl.ds(pl.multiple_of(other * size, 8), size)],
                dst_ref=dst.at[pl.ds(pl.multiple_of(other * size, 8), size)],
                send_sem=ss.at[other],
                recv_sem=rs.at[other],
                device_id=device,
                device_id_type=MESH,
            ).wait_recv()

    def sent(copies):
        for copy in copies:
            copy.wait_send()

    xa = ("lon", lo, n_lon, x_rows, x_send, x_recv, x_ss, x_rs)
    out_going = exchange(*xa)
    arrive(*xa)

    def by_row(count, jumps, per_v):
        r = lax.broadcasted_iota(jnp.int32, (count, 128), 0)
        out = jnp.broadcast_to(per_v[0], (count, 128))
        for v in (1, 2):
            inside = (r >= v * jumps) & (r < (v + 1) * jumps)
            out = jnp.where(inside, jnp.broadcast_to(per_v[v], (count, 128)), out)
        return out

    def scan_states(n, s, t, an, a):
        s_in, total = [], jnp.zeros_like(s[0])
        for e in range(n):
            s_in.append(total)
            total = an * total + s[e]
        t_in, total = [None] * n, -a * total
        for e in reversed(range(n)):
            t_in[e] = total
            total = t[e] + an * total
        return s_in, t_in

    cx = 3 * groups
    a_r = by_row(cx, groups, decay)
    an_r = by_row(cx, groups, [power(v, cols) for v in range(3)])
    g1_r = by_row(cx, groups, [through(v, cols)[0] for v in range(3)])
    g2_r = by_row(cx, groups, [through(v, cols)[1] for v in range(3)])
    p0 = [x_recv[pl.ds(e * x_rows, cx, stride=2), :] for e in range(n_lon)]
    p1 = [x_recv[pl.ds(e * x_rows + 1, cx, stride=2), :] for e in range(n_lon)]
    s_in, t_in = scan_states(n_lon, p0, p1, an_r, a_r)
    sr = [swap(x) for x in s_in]
    tr = [swap(x) for x in t_in]
    s_in2, t_in2 = scan_states(
        n_lon,
        [p0[e] + g1_r * sr[e] + g2_r * tr[e] for e in range(n_lon)],
        [p1[e] + g1_r * tr[e] + g2_r * sr[e] for e in range(n_lon)],
        an_r,
        a_r,
    )
    for e in range(n_lon):
        x_back[pl.ds(e * x_rows, cx, stride=2), :] = pick(s_in[e], s_in2[e])
        x_back[pl.ds(e * x_rows + 1, cx, stride=2), :] = pick(t_in[e], t_in2[e])

    xb = ("lon", lo, n_lon, x_rows, x_back, x_home, xb_ss, xb_rs)
    out_going += exchange(*xb)
    arrive(*xb)

    def home(i):
        return rows_of(
            [
                x_home[pl.ds((v * groups + g) * 2 + i, 8, stride=x_rows), :]
                for v in range(3)
                for g in range(groups)
            ]
        )

    q0, q1 = home(0), home(1)
    q0r, q1r = swap(q0), swap(q1)
    si, s2i = pick(q0, q0r), pick(q0r, q0)
    ti, t2i = pick(q1, q1r), pick(q1r, q1)
    s_en = pick(si, s1r + ah * si)
    t_en = pick(t1r + ah * ti, ti)
    s_own = s2 + g1 * s_en + g2 * t_en
    t_own = t2 + g1 * t_en + g2 * s_en
    s2_en = pick(s2i, swap(s_own) + ah * s2i)
    t2_en = pick(swap(t_own) + ah * t2i, t2i)
    side = pick(s2i + ax * (t_own + ah * t2_en), ax * (s_own + ah * s2_en) + t2i)[:rows]
    yf[pl.ds(half, rows, stride=y_stride), :] = side
    for z in range(1, 8):
        yf[pl.ds(half + z, rows, stride=y_stride), :] = jnp.zeros((rows, 128), F32)

    xu[pl.ds(0, full), :] = s_en
    xu[pl.ds(full, full), :] = t_en
    xu[pl.ds(2 * full, full), :] = s2_en
    xu[pl.ds(3 * full, full), :] = t2_en

    def x_correct(j, _):
        for v in range(3):
            f0 = xtab[pl.ds(v * half + j, 1), :]
            b0 = xtab[pl.ds(v * half + half - 1 - j, 1), :]
            f1 = xtab[pl.ds((3 + v) * half + j, 1), :]
            b1 = xtab[pl.ds((3 + v) * half + half - 1 - j, 1), :]
            at = v * rows
            value = block(xs, j * full + at)
            value = value + xu[pl.ds(at, rows), :] * f1 + xu[pl.ds(full + at, rows), :] * b1
            value = value + xu[pl.ds(2 * full + at, rows), :] * f0 + xu[pl.ds(3 * full + at, rows), :] * b0
            yf[pl.ds(v_base[v] + j, rows, stride=y_stride), :] = value
        return 0

    lax.fori_loop(0, half, x_correct, 0, unroll=2)

    heights = (half + 8, half, half)

    def y_line(ref, i, v):
        return ref[pl.ds(pl.multiple_of(i * y_stride + v_base[v], 8), heights[v]), :]

    def put_y(ref, i, v, value):
        ref[pl.ds(pl.multiple_of(i * y_stride + v_base[v], 8), heights[v]), :] = value

    zero_y = tuple(jnp.zeros((h, 128), F32) for h in heights)

    def y_forward(src):
        def step(i, s):
            new = []
            for v in range(3):
                x = decay[v] * s[v] + y_line(src, i, v)
                put_y(ys, i, v, x)
                new.append(x)
            return tuple(new)

        return lax.fori_loop(0, rows, step, zero_y, unroll=2)

    def y_backward(src, dst):
        def step(q, t):
            i = rows - 1 - q
            new = []
            for v in range(3):
                x = decay[v] * t[v]
                put_y(dst, i, v, y_line(ys, i, v) + x)
                new.append(y_line(src, i, v) + x)
            return tuple(new)

        return lax.fori_loop(0, rows, step, zero_y, unroll=2)

    y_s1 = y_forward(yf)
    y_t1 = y_backward(yf, yu)
    y_s2 = y_forward(yu)
    y_t2 = y_backward(yu, ys)

    for k, states in enumerate((y_s1, y_t1, y_s2, y_t2)):
        for v in range(3):
            for q in range(jj_n):
                y_send[pl.ds((v * jj_n + q) * 4 + k, n_lat, stride=y_rows), :] = states[v][
                    q * n_lat : (q + 1) * n_lat
                ]
        last = 3 * jj_n * 4 + k
        y_send[pl.ds(last, n_lat, stride=y_rows), :] = jnp.zeros((n_lat, 128), F32)
        y_send[pl.ds(last, 1), :] = states[0][half : half + 1]

    ya = ("lat", la, n_lat, y_rows, y_send, y_recv, y_ss, y_rs)
    out_going += exchange(*ya)
    arrive(*ya)

    cy = 3 * jj_n + 1
    a_r = by_row(cy, jj_n, decay)
    an_r = by_row(cy, jj_n, [power(v, rows) for v in range(3)])
    g1_r = by_row(cy, jj_n, [through(v, rows)[0] for v in range(3)])
    g2_r = by_row(cy, jj_n, [through(v, rows)[1] for v in range(3)])

    def got(k):
        return [y_recv[pl.ds(e * y_rows + k, cy, stride=4), :] for e in range(n_lat)]

    s_in, t_in = scan_states(n_lat, got(0), got(1), an_r, a_r)
    for e in range(n_lat):
        y_back[pl.ds(e * y_rows, cy, stride=4), :] = s_in[e]
        y_back[pl.ds(e * y_rows + 1, cy, stride=4), :] = t_in[e]
    p2, p3 = got(2), got(3)
    s_in2, t_in2 = scan_states(
        n_lat,
        [p2[e] + g1_r * s_in[e] + g2_r * t_in[e] for e in range(n_lat)],
        [p3[e] + g1_r * t_in[e] + g2_r * s_in[e] for e in range(n_lat)],
        an_r,
        a_r,
    )
    for e in range(n_lat):
        y_back[pl.ds(e * y_rows + 2, cy, stride=4), :] = s_in2[e]
        y_back[pl.ds(e * y_rows + 3, cy, stride=4), :] = t_in2[e]

    yb = ("lat", la, n_lat, y_rows, y_back, y_home, yb_ss, yb_rs)
    out_going += exchange(*yb)
    arrive(*yb)

    def y_entering(v, k):
        parts = [
            y_home[pl.ds((v * jj_n + q) * 4 + k, n_lat, stride=y_rows), :] for q in range(jj_n)
        ]
        if v == 0:
            last = 3 * jj_n * 4 + k
            parts.append(jnp.broadcast_to(y_home[pl.ds(last, 1), :], (8, 128)))
        return rows_of(parts)

    for v in range(3):
        s_en, t_en, s2_en, t2_en = (y_entering(v, k) for k in range(4))
        if v == 0:
            g1v, g2v = through(0, rows)
            an = power(0, rows)
            first = s2_en + decay[0] * (y_t2[0] + g1v * t_en + g2v * s_en + an * t2_en)
            after = decay[0] * (y_s2[0] + g1v * s_en + g2v * t_en + an * s2_en) + t2_en
            edge_rows[pl.ds(0, half), :] = first[:half]
            edge_rows[pl.ds(half, half), :] = after[:half]

        def y_correct(i, _, v=v, s_en=s_en, t_en=t_en, s2_en=s2_en, t2_en=t2_en):
            f0 = ytab[pl.ds(v * rows + i, 1), :]
            b0 = ytab[pl.ds(v * rows + rows - 1 - i, 1), :]
            f1 = ytab[pl.ds((3 + v) * rows + i, 1), :]
            b1 = ytab[pl.ds((3 + v) * rows + rows - 1 - i, 1), :]
            value = y_line(ys, i, v) + s_en * f1 + t_en * b1
            put_y(yf, i, v, value + s2_en * f0 + t2_en * b0)
            return 0

        lax.fori_loop(0, rows, y_correct, 0)

    def mix_out(b, acc):
        js = batch(b)
        acc = list(acc)
        z0 = None
        for v in range(3):
            parts = []
            for j in js:
                x = yf[pl.ds(v_base[v] + j, rows, stride=y_stride), :]
                acc[v] = acc[v] + x * block(w, (j * 3 + v) * rows)
                parts.append(x)
            y = split_product(rows_of(parts), mats[3 + v])
            tile = sig[pl.ds(v * rows, rows), :]
            zs = [y[t * rows : (t + 1) * rows] * spread(tile, j) for t, j in enumerate(js)]
            for t, j in enumerate(js):
                if v == 0:
                    put_block(temp, (j + 1) * rows, zs[t])
                elif v == 1:
                    put_block(w, (j * 3 + 1) * rows, zs[t] + coupling * z0[t])
                else:
                    put_block(w, (j * 3 + 2) * rows, zs[t])
            if v == 0:
                z0 = zs
        return tuple(acc)

    zero_b = jnp.zeros((rows, 128), F32)
    acc = lax.fori_loop(0, half // 8, mix_out, (zero_b, zero_b, zero_b))

    e_send[...] = jnp.zeros_like(e_send)
    for v in range(3):
        e_send[pl.ds(v, 1), :] = jnp.sum(acc[v], axis=0, keepdims=True)

    def gather_start(axis, me, n, src, dst, ss, rs):
        copies = []
        for o in range(1, n):
            other = lax.rem(me + o, n)
            device = (other, lo) if axis == "lat" else (la, other)
            copy = pltpu.make_async_remote_copy(
                src_ref=src,
                dst_ref=dst.at[pl.ds(pl.multiple_of(me * 8, 8), 8)],
                send_sem=ss.at[other],
                recv_sem=rs.at[me],
                device_id=device,
                device_id_type=MESH,
            )
            copy.start()
            copies.append(copy)
        dst[pl.ds(pl.multiple_of(me * 8, 8), 8), :] = src[...]
        return copies

    def gather_sum(axis, me, n, src, dst, ss, rs):
        for o in range(1, n):
            other = lax.rem(me + o, n)
            device = (other, lo) if axis == "lat" else (la, other)
            pltpu.make_async_remote_copy(
                src_ref=src,
                dst_ref=dst.at[pl.ds(pl.multiple_of(other * 8, 8), 8)],
                send_sem=ss.at[other],
                recv_sem=rs.at[other],
                device_id=device,
                device_id_type=MESH,
            ).wait_recv()
        total = dst[pl.ds(0, 8), :]
        for e in range(1, n):
            total = total + dst[pl.ds(e * 8, 8), :]
        return total

    ea = ("lat", la, n_lat, e_send, e_recv, e_ss, e_rs)
    out_going += gather_start(*ea)

    sig_down = halo_recv[pl.ds(half, rows), :] * has_down
    sig_up = halo_recv[pl.ds(msg_r + half, rows), :] * has_up
    sig_right = halo_recv[pl.ds(2 * msg_r + rows, rows), :] * has_right
    sig_left = halo_recv[pl.ds(2 * msg_r + msg_c + rows, rows), :] * has_left
    wide = jnp.broadcast_to(low1, (half, 128))

    def row_sigma(tile, r):
        t = jnp.concatenate([tile, jnp.zeros((128 - rows, 128), F32)], axis=0).T
        a = jnp.broadcast_to(t[:half, r : r + 1], (half, 128))
        b = jnp.broadcast_to(t[half : 2 * half, r : r + 1], (half, 128))
        return jnp.where(wide, a, b)

    edges = split_product(
        rows_of([edge_rows[...], yf[pl.ds(half, rows, stride=y_stride), :]]), mats[3]
    )
    edge_rows[pl.ds(0, half), :] = edges[:half] * row_sigma(sig_up, rows - 1)
    edge_rows[pl.ds(half, half), :] = edges[half : 2 * half] * row_sigma(sig_down, 0)
    lane_r = lax.broadcasted_iota(jnp.int32, (rows, 128), 1)
    side_sig = jnp.where(
        lane_r < 64,
        jnp.take_along_axis(sig_left, jnp.full((rows, 128), cols - 1), axis=1, mode="promise_in_bounds"),
        jnp.take_along_axis(sig_right, jnp.zeros((rows, 128), jnp.int32), axis=1, mode="promise_in_bounds"),
    )
    side = edges[2 * half :] * side_sig
    close_columns(side, side)

    def unpair(v, js, values):
        for t in range(0, len(js), 2):
            even, odd = values[t], values[t + 1]
            k = lax.div(js[t], 2)
            out_ref[v, :, pl.ds(pl.multiple_of(k * 128, 128), 128)] = pick(even, swap(odd))
            out_ref[v, :, pl.ds(pl.multiple_of((k + half // 2) * 128, 128), 128)] = pick(swap(even), odd)

    def finish(b, _):
        js = batch(b)
        y = split_product(rows_of([laplace(j) for j in js]), mats[7])
        unpair(0, js, [block(temp, (j + 1) * rows) for j in js])
        unpair(1, js, [block(w, (j * 3 + 1) * rows) for j in js])
        unpair(
            2,
            js,
            [y[t * rows : (t + 1) * rows] + block(w, (j * 3 + 2) * rows) for t, j in enumerate(js)],
        )
        return 0

    lax.fori_loop(0, half // 8, finish, 0)

    f_send[...] = gather_sum(*ea)
    fa = ("lon", lo, n_lon, f_send, f_recv, f_ss, f_rs)
    out_going += gather_start(*fa)
    total = gather_sum(*fa)
    total = total + swap(total)

    rank = (la * n_lon + lo).astype(F32)
    keep = lane[:1] < 64
    strict = (
        lax.broadcasted_iota(jnp.int32, (128, 128), 0) < lax.broadcasted_iota(jnp.int32, (128, 128), 1)
    ).astype(F32)
    before = jnp.zeros((1, 1), F32)
    outs = [jnp.zeros((1, 1), F32)] * 3
    scale = 1.0 / float(rows * n_lat * cols * n_lon)
    for v in range(3):
        mine = jnp.where(keep & (small[4 + v : 5 + v] == rank), 1.0, 0.0)
        slot = jnp.dot(jnp.broadcast_to(mine, (8, 128)), strict, preferred_element_type=F32)[:1] + before
        before = before + jnp.sum(mine, axis=1, keepdims=True)
        value = total[v : v + 1] * gain[v] * scale * mine
        for k in range(3):
            outs[k] = outs[k] + jnp.sum(jnp.where(slot == float(k), value, 0.0), axis=1, keepdims=True)
    l8 = lane[:1]
    row = jnp.where(l8 == 0, outs[0], jnp.where(l8 == 1, outs[1], outs[2]))
    energy_ref[...] = row

    sent(out_going)


def shards(state, sigma, vert, bal_temp, chi_coef, scales, classes, owner):
    n_lat = lax.axis_size("lat")
    n_lon = lax.axis_size("lon")
    rows, cols = state.shape[1], sigma.shape[2]
    half = cols // 2
    ids = jnp.arange(scales.shape[0], dtype=jnp.int32)
    length = jnp.sum(jnp.where(classes[:, None] == ids[None, :], scales[None, :], 0.0), axis=1)
    small = jnp.concatenate(
        [length.reshape(3, 64), chi_coef.reshape(1, 64), owner.astype(F32).reshape(3, 64), jnp.ones((1, 64), F32)]
    )
    small = jnp.concatenate([small, small], axis=1)
    jj_n = half // n_lat
    y_rows = 3 * jj_n * 4 + 4
    y_stride = 3 * half + 8
    halo_rows = 2 * (half + rows) + 4 * rows
    vm = lambda r, d=F32: pltpu.VMEM((r, 128), d)
    dma = lambda n: pltpu.SemaphoreType.DMA((n,))
    body = functools.partial(kernel, (n_lat, n_lon, rows, cols))
    spec = pl.BlockSpec(memory_space=pltpu.VMEM)
    applied, energy = pl.pallas_call(
        body,
        out_shape=(
            jax.ShapeDtypeStruct(state.shape, F32),
            jax.ShapeDtypeStruct((1, 128), F32),
        ),
        in_specs=[spec] * 5,
        out_specs=(spec, spec),
        scratch_shapes=[
            pltpu.VMEM((8, 256, 256), BF16),
            vm(64),
            vm(3 * rows),
            vm((half + 2) * rows),
            vm(half * 3 * rows),
            vm(half * 3 * rows),
            vm(half * 3 * rows),
            vm(rows * y_stride),
            vm(rows * y_stride),
            vm(rows * y_stride),
            vm(6 * half),
            vm(6 * rows),
            vm(2 * half),
            vm(halo_rows),
            vm(halo_rows),
            vm(n_lon * 24),
            vm(n_lon * 24),
            vm(n_lon * 24),
            vm(n_lon * 24),
            vm(n_lat * y_rows),
            vm(n_lat * y_rows),
            vm(n_lat * y_rows),
            vm(n_lat * y_rows),
            vm(8),
            vm(8 * n_lat),
            vm(8),
            vm(8 * n_lon),
            dma(4),
            dma(4),
        ]
        + [dma(n_lon)] * 4
        + [dma(n_lat)] * 6
        + [dma(n_lon)] * 2,
        compiler_params=pltpu.CompilerParams(
            collective_id=0, has_side_effects=True, vmem_limit_bytes=56 * 1024 * 1024
        ),
    )(state, sigma, vert, bal_temp, small)
    return applied, energy[:, :3]


def solution(mesh):
    return jax.shard_map(
        shards,
        mesh=mesh,
        in_specs=(P(None, "lat", "lon"), P(None, "lat", "lon"), P(), P(), P(), P(), P(), P()),
        out_specs=(P(None, "lat", "lon"), P(("lat", "lon"), None)),
        check_vma=False,
    )
```

time: 383 us -> 61.8 us (0.16)
  the two profiles are of different devices: /device:TPU:3 before, /device:TPU:1 now
where the time goes in v1:
time: 61.8 us; the launch traced here: 61.6 us
  Pallas kernels  54.6 us (88%)
  local copies, waits for them, and re-layouts  3.48 us (6%)
  other arithmetic  2.86 us (5%)
  between operations  0.65 us (1%)
    pallas_call x1, Pallas kernels, shards(): pl.pallas_call(body, out_shape=(jax.ShapeDtypeStruct(state.shape, F32), j...  54.6 us
    unnamed x4, local copies, waits for them, and re-layouts  3.31 us
    concatenate x1, other arithmetic, shards(): small = jnp.concatenate([small, small], axis=1)  1.4 us

profile of v1, /device:TPU:1, one launch (start us, length us, event | category | flops | bytes accessed | tf_op | source)
XLA Modules:
  0.0 61.6 jit_solution(16069395794109822413)
XLA Ops:
  0.6 0.8 %select_reduce_fusion = f32[192]{0:T(256)S(1)} fusion(f32[8]{0:T(128)} %param.13, s32[192]{0:T(256)} %param.14), kind=kLoop, calls=%fused_computation | loop fusion | flops 4416 | bytes 1568 | tf_op jit(solution)/shard_map/reduce_sum | solution.py:711
  1.4 0.1 reshape.15
  1.5 0.7 %convert_element_type.3 = f32[192]{0:T(256)S(1)} convert(s32[192]{0:T(256)} %param.15) | non-fusion elementwise | flops 192 | bytes 1536 | tf_op jit(solution)/shard_map/convert_element_type | solution.py:713
  2.2 0.1 reshape.17
  2.3 1.4 %maximum_maximum_fusion.small_ref = f32[8,128]{1,0:T(8,128)} fusion(f32[1,64]{1,0:T(1,128)S(1)} %broadcast_in_dim.20, f32[3,64]{1,0:T(4,128)S(1)} %reshape.17, f32[1,64]{1,0:T(1,128)} %bitcast.2, f32[3,64]{1,0:T(4,128)S(1)} %reshape.15), kind=kLoop, calls=%fused_computation.2 | loop fusion | flops 7168 | bytes 6144 | tf_op jit(solution)/shard_map/concatenate | solution.py:715
  3.7 54.6 %shard_map.95 = (f32[3,24,6144]{2,1,0:T(8,128)}, f32[1,128]{1,0:T(1,128)}) custom-call(f32[3,24,6144]{2,1,0:T(8,128)} %state_ref.1, f32[3,24,96]{2,1,0:T(8,128)} %sigma_ref.1, f32[3,64,64]{2,1,0:T(8,128)} %vert_ref.1, f32[64,64]{1,0:T(8,128)} %bal_ref.1, f32[8,128]{1,0:T(8,128)} %maximum_maximum_fusion.small_ref), custom_call_target="tpu_custom_call" | custom-call | tf_op jit(solution)/shard_map/pallas_call | solution.py:724
  58.3 0.0 copy-start
  58.3 2.8 %copy.12 = f32[3,24,6144]{2,1,0:T(8,128)} copy(f32[3,24,6144]{2,1,0:T(8,128)} %get-tuple-element.8) | data formatting | bytes 3538944
  61.1 0.0 copy-done
  61.1 0.5 copy.13
  (1 shorter events, 0.0 us)
Async XLA Ops:
  58.3 2.8 %copy-start = (f32[1,128]{1,0:T(1,128)S(1)}, f32[1,128]{1,0:T(1,128)}, u32[]{:S(2)}) copy-start(f32[1,128]{1,0:T(1,128)} %get-tuple-element.5) | copy-start | bytes 1540

commit v2 on v0

v2 whole, which is shorter than its diff:
```python
import functools

import jax
import jax.numpy as jnp
from jax import lax
from jax.experimental import pallas as pl
from jax.experimental.pallas import tpu as pltpu
from jax.sharding import PartitionSpec as P

F32 = jnp.float32
BF16 = jnp.bfloat16
MESH = pl.DeviceIdType.MESH


def split_product(x, w):
    hi = x.astype(BF16)
    lo = (x - hi.astype(F32)).astype(BF16)
    y = jnp.dot(jnp.concatenate([hi, lo], axis=1), w, preferred_element_type=F32)
    return y[:, :128] + y[:, 128:]


def swap(x):
    return pltpu.roll(x, 64, 1)


def rows_of(parts):
    return jnp.concatenate(parts, axis=0)


def layout(n_lat, n_lon, rows, cols, n_class):
    half = cols // 2
    jj_n = half // n_lat
    groups = rows // 8
    spec = {}
    for c, count in enumerate((1, 2)):
        spec[f"x_rows{c}"] = -(-count * groups * 2 // 8) * 8
        spec[f"y_rows{c}"] = -(-(count * jj_n * 4 + (4 if c == 0 else 0)) // 8) * 8
        spec[f"y_stride{c}"] = count * half + (8 if c == 0 else 0)
    shapes = {
        "in_sem": 3,
        "small_sem": 7,
        "halo_ss": 4,
        "halo_rs": 4,
        "e_ss": 1,
        "e_rs": 1,
        "f_ss": 1,
        "f_rs": 1,
    }
    for name in shapes:
        shapes[name] = pltpu.SemaphoreType.DMA((shapes[name],))
    vm = lambda r: pltpu.VMEM((r, 128), F32)
    shapes["state"] = pltpu.VMEM((3, rows, cols * 64), F32)
    shapes["sigma"] = pltpu.VMEM((3, rows, cols), F32)
    shapes["vert"] = pltpu.VMEM((3, 64, 64), F32)
    shapes["bal"] = pltpu.VMEM((64, 64), F32)
    shapes["chi"] = pltpu.VMEM((1, 64), F32)
    shapes["scales"] = pltpu.VMEM((1, n_class), F32)
    shapes["classes"] = pltpu.VMEM((1, 192), jnp.int32)
    shapes["owner"] = pltpu.VMEM((1, 192), jnp.int32)
    shapes["mats"] = pltpu.VMEM((8, 256, 256), BF16)
    sizes = {
        "table": 8,
        "pad": 64,
        "sig": 3 * rows,
        "temp": (half + 2) * rows,
        "xtab": 6 * half,
        "ytab": 6 * rows,
        "edge_rows": 2 * half,
        "halo_send": 2 * (half + rows) + 4 * rows,
        "halo_recv": 2 * (half + rows) + 4 * rows,
        "e_send": 8,
        "e_recv": 8 * n_lat,
        "f_send": 8,
        "f_recv": 8 * n_lon,
    }
    for c, count in enumerate((1, 2)):
        for name in ("w", "xs", "xt", "xu", "xv"):
            sizes[f"{name}{c}"] = half * count * rows
        sizes[f"xe{c}"] = 4 * count * rows
        for name in ("yf", "ys", "yt", "yv", "yu"):
            sizes[f"{name}{c}"] = rows * spec[f"y_stride{c}"]
        for name in ("send", "recv", "back", "home"):
            sizes[f"x_{name}{c}"] = n_lon * spec[f"x_rows{c}"]
            sizes[f"y_{name}{c}"] = n_lat * spec[f"y_rows{c}"]
        for name in ("ss", "rs", "bss", "brs"):
            shapes[f"x_{name}{c}"] = pltpu.SemaphoreType.DMA((1,))
            shapes[f"y_{name}{c}"] = pltpu.SemaphoreType.DMA((1,))
    for name, size in sizes.items():
        shapes[name] = vm(size)
    return spec, shapes


CHUNKS = ((0,), (1, 2))


class Names:
    def __init__(self, names, refs):
        for name, ref in zip(names, refs):
            setattr(self, name, ref)

    def at(self, name, c):
        return getattr(self, f"{name}{c}")


def kernel(
    dims,
    spec,
    names,
    state_hbm,
    sigma_hbm,
    vert_hbm,
    bal_hbm,
    chi_hbm,
    scales_hbm,
    class_hbm,
    owner_hbm,
    out_ref,
    energy_ref,
    *refs,
):
    n_lat, n_lon, rows, cols = dims
    half = cols // 2
    jj_n = half // n_lat
    groups = rows // 8
    R = Names(names, refs)
    state_ref, table, mats, pad, sig, temp = R.state, R.table, R.mats, R.pad, R.sig, R.temp
    xtab, ytab, edge_rows = R.xtab, R.ytab, R.edge_rows
    halo_send, halo_recv = R.halo_send, R.halo_recv
    la = lax.axis_index("lat")
    lo = lax.axis_index("lon")

    barrier = pltpu.get_barrier_semaphore()
    for o in range(1, n_lat):
        pl.semaphore_signal(barrier, inc=1, device_id=(lax.rem(la + o, n_lat), lo), device_id_type=MESH)
    for o in range(1, n_lon):
        pl.semaphore_signal(barrier, inc=1, device_id=(la, lax.rem(lo + o, n_lon)), device_id_type=MESH)

    sigma_ref, vert_ref, bal_ref = R.sigma, R.vert, R.bal
    chi_ref, scales_ref, class_ref, owner_ref = R.chi, R.scales, R.classes, R.owner
    small = []
    for i, (src, dst) in enumerate(
        (
            (class_hbm, class_ref),
            (scales_hbm, scales_ref),
            (vert_hbm, vert_ref),
            (bal_hbm, bal_ref),
            (sigma_hbm, sigma_ref),
            (chi_hbm, chi_ref),
            (owner_hbm, owner_ref),
        )
    ):
        small.append(pltpu.make_async_copy(src, dst, R.small_sem.at[i]))
        small[-1].start()
    loads = {}
    for v in (2, 1, 0):
        loads[v] = pltpu.make_async_copy(state_hbm.at[v], state_ref.at[v], R.in_sem.at[v])
        loads[v].start()

    lane = lax.broadcasted_iota(jnp.int32, (8, 128), 1)
    low1 = lane[:1] < 64

    def low(x):
        return jnp.broadcast_to(low1, x.shape)

    def pick(a, b):
        return jnp.where(low(a), a, b)

    for copy in small:
        copy.wait()

    table[...] = jnp.zeros_like(table)

    def levels(row):
        table[0:1, :] = row[:, :128]
        table[1:2, :64] = row[:, 128:]
        pair01 = table[...]
        flip01 = swap(pair01)
        first, second = pick(pair01, flip01), pick(flip01, pair01)
        return [first[0:1], second[0:1], first[1:2]]

    classes = class_ref[...]
    lengths = jnp.zeros(classes.shape, F32)
    for c in range(scales_ref.shape[1]):
        lengths = jnp.where(classes == c, scales_ref[:, c : c + 1], lengths)
    length = levels(lengths)
    owners = levels(owner_ref[...].astype(F32))
    table[0:1, :64] = chi_ref[...]
    coupling = table[...]
    coupling = pick(coupling, swap(coupling))[0:1]
    decay = [jnp.exp(-1.0 / r) for r in length]

    def power(v, k):
        return jnp.exp(-float(k) / length[v])

    def through(v, n):
        a = decay[v]
        return float(n) * power(v, n), a * (1.0 - power(v, 2 * n)) / (1.0 - a * a)

    def fill_table(ref, n):
        pos = lax.broadcasted_iota(jnp.int32, (n, 128), 0).astype(F32)
        for v in range(3):
            a, r = decay[v], length[v]
            first = jnp.exp(-(pos + 1.0) / r)
            tail = 1.0 - jnp.exp(-2.0 * (n - 1.0 - pos) / r)
            second = (pos + 1.0) * first + first * (a * a) * tail / (1.0 - a * a)
            ref[pl.ds(v * n, n), :] = first
            ref[pl.ds((3 + v) * n, n), :] = second

    fill_table(xtab, half)
    fill_table(ytab, rows)

    gain = []
    for v in range(3):
        a = decay[v]
        c = (1.0 - a) / (1.0 + a)
        gain.append(length[v] * jnp.sqrt(length[v]) * (c * c) * (c * c))

    def put_matrix(slot, m):
        pad[:, :64] = m
        top = pad[...]
        full = rows_of([top, swap(top)])
        hi = full.astype(BF16)
        low_part = (full - hi.astype(F32)).astype(BF16)
        mats[slot] = rows_of(
            [
                jnp.concatenate([hi, low_part], axis=1),
                jnp.concatenate([hi, jnp.zeros_like(hi)], axis=1),
            ]
        )

    pad[...] = jnp.zeros_like(pad)
    for v in range(3):
        put_matrix(v, vert_ref[v])
        put_matrix(3 + v, (vert_ref[v] * gain[v][:, :64]).T)
    put_matrix(6, bal_ref[...])
    put_matrix(7, bal_ref[...].T)

    for v in range(3):
        sig[pl.ds(v * rows, rows), :] = jnp.zeros((rows, 128), F32)
        sig[pl.ds(v * rows, rows), :cols] = sigma_ref[v]
    column = jnp.where(lax.broadcasted_iota(jnp.int32, (rows, 128), 1) < 64, 0, half)

    def spread(tile, j):
        return jnp.take_along_axis(tile, column + j, axis=1, mode="promise_in_bounds")

    def block(ref, at):
        return ref[pl.ds(pl.multiple_of(at, 8), rows), :]

    def put_block(ref, at, value):
        ref[pl.ds(pl.multiple_of(at, 8), rows), :] = value


    def pair(v):
        def step(k, _):
            at1 = pl.ds(pl.multiple_of(k * 128, 128), 128)
            at2 = pl.ds(pl.multiple_of((k + half // 2) * 128, 128), 128)
            n1, n2 = state_ref[v, :, at1], state_ref[v, :, at2]
            if v == 0:
                n1 = n1 + coupling * state_ref[1, :, at1]
                n2 = n2 + coupling * state_ref[1, :, at2]
            even = pick(n1, swap(n2))
            odd = pick(swap(n1), n2)
            if v == 2:
                put_block(temp, (2 * k + 1) * rows, even)
                put_block(temp, (2 * k + 2) * rows, odd)
            elif v == 1:
                put_block(R.w1, 4 * k * rows, even)
                put_block(R.w1, (4 * k + 2) * rows, odd)
            else:
                put_block(R.w0, 2 * k * rows, even)
                put_block(R.w0, (2 * k + 1) * rows, odd)
            return 0

        lax.fori_loop(0, half // 2, step, 0, unroll=4)

    def batch(b):
        return [b * 8 + t for t in range(8)]

    def w_at(v, j):
        return j * rows if v == 0 else (2 * j + v - 1) * rows

    def w_ref(v):
        return R.w0 if v == 0 else R.w1

    loads[2].wait()
    pair(2)

    sig0 = sig[pl.ds(0, rows), :]
    msg_r, msg_c = half + rows, 2 * rows
    halo_send[pl.ds(0, half), :] = temp[pl.ds(rows, half, stride=rows), :]
    halo_send[pl.ds(half, rows), :] = sig0
    halo_send[pl.ds(msg_r, half), :] = temp[pl.ds(2 * rows - 1, half, stride=rows), :]
    halo_send[pl.ds(msg_r + half, rows), :] = sig0
    halo_send[pl.ds(2 * msg_r, rows), :] = temp[pl.ds(rows, rows), :]
    halo_send[pl.ds(2 * msg_r + rows, rows), :] = sig0
    halo_send[pl.ds(2 * msg_r + msg_c, rows), :] = temp[pl.ds(half * rows, rows), :]
    halo_send[pl.ds(2 * msg_r + msg_c + rows, rows), :] = sig0

    loads[1].wait()
    pair(1)

    def mix_in(b, _):
        js = batch(b)
        chi = [block(R.w1, w_at(1, j)) for j in js]
        for v, parts in ((1, chi), (2, [block(temp, (j + 1) * rows) for j in js])):
            y = split_product(rows_of(parts), mats[v])
            tile = sig[pl.ds(v * rows, rows), :]
            for t, j in enumerate(js):
                put_block(R.w1, w_at(v, j), y[t * rows : (t + 1) * rows] * spread(tile, j))
        return 0

    lax.fori_loop(0, half // 8, mix_in, 0, unroll=True)

    def tall(per_v):
        return rows_of([jnp.broadcast_to(c, (rows, 128)) for c in per_v])

    def both_ways(n, load, put_s, put_t, times, start):
        def step(q, carry):
            s, t = carry
            r = n - 1 - q
            s = [x + p for x, p in zip(times(s), load(q))]
            put_s(q, s)
            m = times(t)
            put_t(r, m)
            t = [x + p for x, p in zip(m, load(r))]
            return tuple(s), tuple(t)

        return lax.fori_loop(0, n, step, (start, start), unroll=4)

    def x_filter(c):
        vs = CHUNKS[c]
        full = len(vs) * rows
        ax = tall([decay[v] for v in vs])

        def line(ref, j):
            return ref[pl.ds(pl.multiple_of(j * full, 8), full), :]

        def put(ref):
            def go(j, value):
                ref[pl.ds(pl.multiple_of(j * full, 8), full), :] = value[0]

            return go

        w, xs, xt, xu, xv = (R.at(n, c) for n in ("w", "xs", "xt", "xu", "xv"))
        zero = (jnp.zeros((full, 128), F32),)
        times = lambda s: [ax * s[0]]
        (s1,), (t1,) = both_ways(half, lambda j: [line(w, j)], put(xs), put(xt), times, zero)
        second = lambda j: [line(xs, j) + line(xt, j)]
        (s2,), (t2,) = both_ways(half, second, put(xu), put(xv), times, zero)

        ah = tall([power(v, half) for v in vs])
        g1 = tall([through(v, half)[0] for v in vs])
        g2 = tall([through(v, half)[1] for v in vs])
        s1r, t1r, s2r, t2r = swap(s1), swap(t1), swap(s2), swap(t2)
        q0 = pick(ah * s1 + s1r, s2 + g1 * s1r + ah * (s2r + g2 * t1))
        q1 = pick(t1 + ah * t1r, t2r + g1 * t1 + ah * (t2 + g2 * s1r))
        send = R.at("x_send", c)
        for i, q in enumerate((q0, q1)):
            for g in range(full // 8):
                send[pl.ds(g * 2 + i, 8, stride=spec[f"x_rows{c}"]), :] = q[g * 8 : g * 8 + 8]
        return dict(s1r=s1r, t1r=t1r, s2=s2, t2=t2, ah=ah, g1=g1, g2=g2, ax=ax)

    def remote(axis, other, src, dst, ss, rs):
        device = (other, lo) if axis == "lat" else (la, other)
        return pltpu.make_async_remote_copy(
            src_ref=src,
            dst_ref=dst,
            send_sem=ss.at[0],
            recv_sem=rs.at[0],
            device_id=device,
            device_id_type=MESH,
        )

    def part(ref, slot, size):
        return ref.at[pl.ds(pl.multiple_of(slot * size, 8), size)]

    def way(axis, c, back):
        me, n = (la, n_lat) if axis == "lat" else (lo, n_lon)
        k = "y" if axis == "lat" else "x"
        size = spec[f"{k}_rows{c}"]
        a, b, ss, rs = ("back", "home", "bss", "brs") if back else ("send", "recv", "ss", "rs")
        return axis, me, n, size, *(R.at(f"{k}_{name}", c) for name in (a, b, ss, rs))

    def exchange(axis, me, n, size, src, dst, ss, rs, shared=False):
        for o in range(1, n):
            other = lax.rem(me + o, n)
            remote(axis, other, src if shared else part(src, other, size), part(dst, me, size), ss, rs).start()
        pltpu.make_async_copy(src if shared else part(src, me, size), part(dst, me, size), rs.at[0]).start()

    def arrive(axis, me, n, size, src, dst, ss, rs, shared=False):
        remote(axis, lax.rem(me + 1, n), dst, dst, ss, rs).wait_recv()

    def left_for_good(axis, me, n, size, src, dst, ss, rs):
        gone = dst.at[pl.ds(0, (n - 1) * size)]
        remote(axis, lax.rem(me + 1, n), gone, gone, ss, rs).wait_send()

    def by_row(count, jumps, per_v):
        r = lax.broadcasted_iota(jnp.int32, (count, 128), 0)
        out = jnp.broadcast_to(per_v[0], (count, 128))
        for v in range(1, len(per_v)):
            inside = (r >= v * jumps) & (r < (v + 1) * jumps)
            out = jnp.where(inside, jnp.broadcast_to(per_v[v], (count, 128)), out)
        return out

    def scan_states(n, s, t, an, a):
        s_in, total = [], jnp.zeros_like(s[0])
        for e in range(n):
            s_in.append(total)
            total = an * total + s[e]
        t_in, total = [None] * n, -a * total
        for e in reversed(range(n)):
            t_in[e] = total
            total = t[e] + an * total
        return s_in, t_in

    def scan_coefs(vs, count, jumps, n):
        return (
            by_row(count, jumps, [decay[v] for v in vs]),
            by_row(count, jumps, [power(v, n) for v in vs]),
            by_row(count, jumps, [through(v, n)[0] for v in vs]),
            by_row(count, jumps, [through(v, n)[1] for v in vs]),
        )

    def x_scan(c):
        vs = CHUNKS[c]
        count, size = len(vs) * groups, spec[f"x_rows{c}"]
        a_r, an_r, g1_r, g2_r = scan_coefs(vs, count, groups, cols)
        recv, back = R.at("x_recv", c), R.at("x_back", c)
        p0 = [recv[pl.ds(e * size, count, stride=2), :] for e in range(n_lon)]
        p1 = [recv[pl.ds(e * size + 1, count, stride=2), :] for e in range(n_lon)]
        s_in, t_in = scan_states(n_lon, p0, p1, an_r, a_r)
        sr = [swap(x) for x in s_in]
        tr = [swap(x) for x in t_in]
        s_in2, t_in2 = scan_states(
            n_lon,
            [p0[e] + g1_r * sr[e] + g2_r * tr[e] for e in range(n_lon)],
            [p1[e] + g1_r * tr[e] + g2_r * sr[e] for e in range(n_lon)],
            an_r,
            a_r,
        )
        for e in range(n_lon):
            back[pl.ds(e * size, count, stride=2), :] = pick(s_in[e], s_in2[e])
            back[pl.ds(e * size + 1, count, stride=2), :] = pick(t_in[e], t_in2[e])

    def x_finish(c, k):
        vs = CHUNKS[c]
        full = len(vs) * rows
        stride = spec[f"y_stride{c}"]
        home, yf, xe = R.at("x_home", c), R.at("yf", c), R.at("xe", c)
        xt, xv = R.at("xu", c), R.at("xv", c)

        def got(i):
            return rows_of(
                [home[pl.ds(g * 2 + i, 8, stride=spec[f"x_rows{c}"]), :] for g in range(full // 8)]
            )

        q0, q1 = got(0), got(1)
        q0r, q1r = swap(q0), swap(q1)
        si, s2i = pick(q0, q0r), pick(q0r, q0)
        ti, t2i = pick(q1, q1r), pick(q1r, q1)
        s_en = pick(si, k["s1r"] + k["ah"] * si)
        t_en = pick(k["t1r"] + k["ah"] * ti, ti)
        s_own = k["s2"] + k["g1"] * s_en + k["g2"] * t_en
        t_own = k["t2"] + k["g1"] * t_en + k["g2"] * s_en
        s2_en = pick(s2i, swap(s_own) + k["ah"] * s2i)
        t2_en = pick(swap(t_own) + k["ah"] * t2i, t2i)
        if c == 0:
            ax = k["ax"]
            side = pick(s2i + ax * (t_own + k["ah"] * t2_en), ax * (s_own + k["ah"] * s2_en) + t2i)
            yf[pl.ds(half, rows, stride=stride), :] = side
            for z in range(1, 8):
                yf[pl.ds(half + z, rows, stride=stride), :] = jnp.zeros((rows, 128), F32)
        for i, value in enumerate((s_en, t_en, s2_en, t2_en)):
            xe[pl.ds(i * full, full), :] = value

        def correct(j, _):
            for i, v in enumerate(vs):
                f0 = xtab[pl.ds(v * half + j, 1), :]
                b0 = xtab[pl.ds(v * half + half - 1 - j, 1), :]
                f1 = xtab[pl.ds((3 + v) * half + j, 1), :]
                b1 = xtab[pl.ds((3 + v) * half + half - 1 - j, 1), :]
                at = i * rows
                value = block(xt, j * full + at) + block(xv, j * full + at)
                value = value + xe[pl.ds(at, rows), :] * f1 + xe[pl.ds(full + at, rows), :] * b1
                value = value + xe[pl.ds(2 * full + at, rows), :] * f0 + xe[pl.ds(3 * full + at, rows), :] * b0
                yf[pl.ds(i * half + j, rows, stride=stride), :] = value
            return 0

        lax.fori_loop(0, half, correct, 0, unroll=4)

    def y_parts(c):
        return [(0, half + 8)] if c == 0 else [(0, half), (half, half)]

    def y_filter(c):
        vs = CHUNKS[c]
        stride = spec[f"y_stride{c}"]
        ends = []
        for v, (base, height) in zip(vs, y_parts(c)):

            def line(name, i):
                return R.at(name, c)[pl.ds(pl.multiple_of(i * stride + base, 8), height), :]

            def put(name):
                def go(i, value):
                    R.at(name, c)[pl.ds(pl.multiple_of(i * stride + base, 8), height), :] = value[0]

                return go

            zero = (jnp.zeros((height, 128), F32),)
            times = lambda s: [decay[v] * s[0]]
            (s1,), (t1,) = both_ways(rows, lambda i: [line("yf", i)], put("ys"), put("yt"), times, zero)
            second = lambda i: [line("ys", i) + line("yt", i)]
            (s2,), (t2,) = both_ways(rows, second, put("yv"), put("yu"), times, zero)
            ends.append((s1, t1, s2, t2))
        s1, t1, s2, t2 = zip(*ends)
        send, size = R.at("y_send", c), spec[f"y_rows{c}"]
        for k, states in enumerate((s1, t1, s2, t2)):
            for i in range(len(vs)):
                for q in range(jj_n):
                    send[pl.ds((i * jj_n + q) * 4 + k, n_lat, stride=size), :] = states[i][
                        q * n_lat : (q + 1) * n_lat
                    ]
            if c == 0:
                last = jj_n * 4 + k
                send[pl.ds(last, n_lat, stride=size), :] = jnp.zeros((n_lat, 128), F32)
                send[pl.ds(last, 1), :] = states[0][half : half + 1]
        return s2, t2

    def y_scan(c):
        vs = CHUNKS[c]
        count, size = len(vs) * jj_n + (1 if c == 0 else 0), spec[f"y_rows{c}"]
        jumps = jj_n if c else count
        a_r, an_r, g1_r, g2_r = scan_coefs(vs, count, jumps, rows)
        recv, back = R.at("y_recv", c), R.at("y_back", c)

        def got(k):
            return [recv[pl.ds(e * size + k, count, stride=4), :] for e in range(n_lat)]

        def give(k, values):
            for e in range(n_lat):
                back[pl.ds(e * size + k, count, stride=4), :] = values[e]

        s_in, t_in = scan_states(n_lat, got(0), got(1), an_r, a_r)
        give(0, s_in)
        give(1, t_in)
        p2, p3 = got(2), got(3)
        s_in2, t_in2 = scan_states(
            n_lat,
            [p2[e] + g1_r * s_in[e] + g2_r * t_in[e] for e in range(n_lat)],
            [p3[e] + g1_r * t_in[e] + g2_r * s_in[e] for e in range(n_lat)],
            an_r,
            a_r,
        )
        give(2, s_in2)
        give(3, t_in2)

    def y_finish(c, s2, t2):
        home, size = R.at("y_home", c), spec[f"y_rows{c}"]
        for i, v in enumerate(CHUNKS[c]):

            def entering(k):
                parts = [home[pl.ds((i * jj_n + q) * 4 + k, n_lat, stride=size), :] for q in range(jj_n)]
                if c == 0:
                    parts.append(jnp.broadcast_to(home[pl.ds(jj_n * 4 + k, 1), :], (8, 128)))
                return rows_of(parts)

            s_en, t_en, s2_en, t2_en = (entering(k) for k in range(4))
            if c == 0:
                g1v, g2v = through(0, rows)
                an = power(0, rows)
                first = s2_en + decay[0] * (t2[0] + g1v * t_en + g2v * s_en + an * t2_en)
                after = decay[0] * (s2[0] + g1v * s_en + g2v * t_en + an * s2_en) + t2_en
                edge_rows[pl.ds(0, half), :] = first[:half]
                edge_rows[pl.ds(half, half), :] = after[:half]
            base, height = y_parts(c)[i]
            stride = spec[f"y_stride{c}"]
            yt, yv, yf = R.at("yu", c), R.at("yv", c), R.at("yf", c)

            def correct(n, _):
                at = pl.ds(pl.multiple_of(n * stride + base, 8), height)
                f0 = ytab[pl.ds(v * rows + n, 1), :]
                b0 = ytab[pl.ds(v * rows + rows - 1 - n, 1), :]
                f1 = ytab[pl.ds((3 + v) * rows + n, 1), :]
                b1 = ytab[pl.ds((3 + v) * rows + rows - 1 - n, 1), :]
                value = yt[at, :] + yv[at, :] + s_en * f1 + t_en * b1
                yf[at, :] = value + s2_en * f0 + t2_en * b0
                return 0

            lax.fori_loop(0, rows, correct, 0, unroll=2)

    def mix_out(c):
        yf, stride = R.at("yf", c), spec[f"y_stride{c}"]

        def step(b, acc):
            js = batch(b)
            acc = list(acc)
            for i, v in enumerate(CHUNKS[c]):
                parts = []
                for j in js:
                    x = yf[pl.ds(i * half + j, rows, stride=stride), :]
                    acc[i] = acc[i] + x * block(w_ref(v), w_at(v, j))
                    parts.append(x)
                y = split_product(rows_of(parts), mats[3 + v])
                tile = sig[pl.ds(v * rows, rows), :]
                for t, j in enumerate(js):
                    z = y[t * rows : (t + 1) * rows] * spread(tile, j)
                    if v == 0:
                        put_block(temp, (j + 1) * rows, z)
                    else:
                        put_block(R.w1, w_at(v, j), z)
            return tuple(acc)

        start = tuple(jnp.zeros((rows, 128), F32) for _ in CHUNKS[c])
        acc = lax.fori_loop(0, half // 8, step, start, unroll=True)
        for i, v in enumerate(CHUNKS[c]):
            R.e_send[pl.ds(v, 1), :] = jnp.sum(acc[i], axis=0, keepdims=True)

    kept = {1: x_filter(1)}
    pl.semaphore_wait(barrier, n_lat + n_lon - 2)

    up = (lax.rem(la + n_lat - 1, n_lat), lo)
    down = (lax.rem(la + 1, n_lat), lo)
    left = (la, lax.rem(lo + n_lon - 1, n_lon))
    right = (la, lax.rem(lo + 1, n_lon))
    starts = (0, msg_r, 2 * msg_r, 2 * msg_r + msg_c)
    sizes = (msg_r, msg_r, msg_c, msg_c)
    halo = []
    for q, device in enumerate((up, down, left, right)):
        here = pl.ds(starts[q], sizes[q])
        copy = pltpu.make_async_remote_copy(
            src_ref=halo_send.at[here],
            dst_ref=halo_recv.at[here],
            send_sem=R.halo_ss.at[q],
            recv_sem=R.halo_rs.at[q],
            device_id=device,
            device_id_type=MESH,
        )
        copy.start()
        halo.append(copy)
    xa1, xb1, xa0, xb0 = way("lon", 1, False), way("lon", 1, True), way("lon", 0, False), way("lon", 0, True)
    ya1, yb1, ya0, yb0 = way("lat", 1, False), way("lat", 1, True), way("lat", 0, False), way("lat", 0, True)
    exchange(*xa1)

    loads[0].wait()
    pair(0)
    edge_rows[...] = jnp.zeros_like(edge_rows)

    def close_columns(lo_edge, hi_edge):
        put_block(temp, 0, pick(lo_edge, swap(temp[pl.ds(half * rows, rows), :])))
        put_block(temp, (half + 1) * rows, pick(swap(temp[pl.ds(rows, rows), :]), hi_edge))

    zero_block = jnp.zeros((rows, 128), F32)
    close_columns(zero_block, zero_block)
    row_id = lax.broadcasted_iota(jnp.int32, (rows, 128), 0)

    def laplace(j):
        x = block(temp, (j + 1) * rows)
        above = jnp.where(row_id == 0, edge_rows[pl.ds(j, 1), :], pltpu.roll(x, 1, 0))
        below = jnp.where(row_id == rows - 1, edge_rows[pl.ds(half + j, 1), :], pltpu.roll(x, rows - 1, 0))
        return 4.0 * x - above - below - block(temp, j * rows) - block(temp, (j + 2) * rows)

    def mix_psi(b, _):
        js = batch(b)
        y = split_product(rows_of([laplace(j) for j in js]), mats[6])
        y = y + rows_of([block(R.w0, j * rows) for j in js])
        y = split_product(y, mats[0])
        for t, j in enumerate(js):
            put_block(R.w0, j * rows, y[t * rows : (t + 1) * rows] * spread(sig0, j))
        return 0

    lax.fori_loop(0, half // 8, mix_psi, 0, unroll=True)

    wide = jnp.broadcast_to(low1, (half, 128))

    def row_sigma(tile, r):
        t = jnp.concatenate([tile, jnp.zeros((128 - rows, 128), F32)], axis=0).T
        a = jnp.broadcast_to(t[:half, r : r + 1], (half, 128))
        b = jnp.broadcast_to(t[half : 2 * half, r : r + 1], (half, 128))
        return jnp.where(wide, a, b)

    lane_r = lax.broadcasted_iota(jnp.int32, (rows, 128), 1)

    def side_sigma(a, at_a, b, at_b):
        take = lambda x, at: jnp.take_along_axis(
            x, jnp.full((rows, 128), at, jnp.int32), axis=1, mode="promise_in_bounds"
        )
        return jnp.where(lane_r < 64, take(a, at_a), take(b, at_b))

    own_up, own_down = row_sigma(sig0, 0), row_sigma(sig0, rows - 1)
    own_side = side_sigma(sig0, 0, sig0, cols - 1)

    arrive(*xa1)
    x_scan(1)
    exchange(*xb1)

    for copy in halo:
        copy.wait()
    has_up = jnp.where(la > 0, 1.0, 0.0).astype(F32)
    has_down = jnp.where(la < n_lat - 1, 1.0, 0.0).astype(F32)
    has_left = jnp.where(lo > 0, 1.0, 0.0).astype(F32)
    has_right = jnp.where(lo < n_lon - 1, 1.0, 0.0).astype(F32)
    from_right = swap(halo_recv[pl.ds(2 * msg_r, rows), :]) * has_right
    from_left = swap(halo_recv[pl.ds(2 * msg_r + msg_c, rows), :]) * has_left
    outside = rows_of(
        [
            halo_recv[pl.ds(msg_r, half), :] * has_up,
            halo_recv[pl.ds(0, half), :] * has_down,
            pick(from_left, from_right),
        ]
    )
    outside = split_product(split_product(outside, mats[6]), mats[0])
    first_rows = pl.ds(0, half, stride=rows)
    last_rows = pl.ds(rows - 1, half, stride=rows)
    R.w0[first_rows, :] = R.w0[first_rows, :] - outside[:half] * own_up
    R.w0[last_rows, :] = R.w0[last_rows, :] - outside[half : 2 * half] * own_down
    side = outside[2 * half :] * own_side
    at_last = pl.ds((half - 1) * rows, rows)
    R.w0[pl.ds(0, rows), :] = R.w0[pl.ds(0, rows), :] - pick(side, zero_block)
    R.w0[at_last, :] = R.w0[at_last, :] - pick(zero_block, side)

    kept[0] = x_filter(0)
    exchange(*xa0)

    arrive(*xb1)
    arrive(*xa0)
    x_scan(0)
    exchange(*xb0)
    x_finish(1, kept[1])
    ends1 = y_filter(1)
    exchange(*ya1)
    arrive(*xb0)
    x_finish(0, kept[0])
    ends0 = y_filter(0)
    exchange(*ya0)

    up_sigma = row_sigma(halo_recv[pl.ds(msg_r + half, rows), :] * has_up, rows - 1)
    down_sigma = row_sigma(halo_recv[pl.ds(half, rows), :] * has_down, 0)
    side_out = side_sigma(
        halo_recv[pl.ds(2 * msg_r + msg_c + rows, rows), :] * has_left,
        cols - 1,
        halo_recv[pl.ds(2 * msg_r + rows, rows), :] * has_right,
        0,
    )

    arrive(*ya1)
    y_scan(1)
    exchange(*yb1)
    arrive(*ya0)
    y_scan(0)
    exchange(*yb0)

    R.e_send[...] = jnp.zeros_like(R.e_send)
    arrive(*yb1)
    y_finish(1, *ends1)
    mix_out(1)
    arrive(*yb0)
    y_finish(0, *ends0)
    mix_out(0)
    ea = ("lat", la, n_lat, 8, R.e_send, R.e_recv, R.e_ss, R.e_rs)
    exchange(*ea, shared=True)

    edges = split_product(
        rows_of([edge_rows[...], R.yf0[pl.ds(half, rows, stride=spec["y_stride0"]), :]]), mats[3]
    )
    edge_rows[pl.ds(0, half), :] = edges[:half] * up_sigma
    edge_rows[pl.ds(half, half), :] = edges[half : 2 * half] * down_sigma
    side = edges[2 * half :] * side_out
    close_columns(side, side)

    def unpair(v, js, values):
        for t in range(0, len(js), 2):
            even, odd = values[t], values[t + 1]
            k = lax.div(js[t], 2)
            out_ref[v, :, pl.ds(pl.multiple_of(k * 128, 128), 128)] = pick(even, swap(odd))
            out_ref[v, :, pl.ds(pl.multiple_of((k + half // 2) * 128, 128), 128)] = pick(swap(even), odd)

    def finish(b, _):
        js = batch(b)
        y = split_product(rows_of([laplace(j) for j in js]), mats[7])
        z0 = [block(temp, (j + 1) * rows) for j in js]
        unpair(0, js, z0)
        unpair(1, js, [block(R.w1, w_at(1, j)) + coupling * z for j, z in zip(js, z0)])
        unpair(2, js, [y[t * rows : (t + 1) * rows] + block(R.w1, w_at(2, j)) for t, j in enumerate(js)])
        return 0

    lax.fori_loop(0, half // 8, finish, 0, unroll=True)

    def total_of(ref, n):
        total = ref[pl.ds(0, 8), :]
        for e in range(1, n):
            total = total + ref[pl.ds(e * 8, 8), :]
        return total

    arrive(*ea, shared=True)
    R.f_send[...] = total_of(R.e_recv, n_lat)
    fa = ("lon", lo, n_lon, 8, R.f_send, R.f_recv, R.f_ss, R.f_rs)
    exchange(*fa, shared=True)
    arrive(*fa, shared=True)
    total = total_of(R.f_recv, n_lon)
    total = total + swap(total)

    rank = (la * n_lon + lo).astype(F32)
    keep = lane[:1] < 64
    strict = (
        lax.broadcasted_iota(jnp.int32, (128, 128), 0) < lax.broadcasted_iota(jnp.int32, (128, 128), 1)
    ).astype(F32)
    before = jnp.zeros((1, 1), F32)
    outs = [jnp.zeros((1, 1), F32)] * 3
    scale = 1.0 / float(rows * n_lat * cols * n_lon)
    for v in range(3):
        mine = jnp.where(keep & (owners[v] == rank), 1.0, 0.0)
        slot = jnp.dot(jnp.broadcast_to(mine, (8, 128)), strict, preferred_element_type=F32)[:1] + before
        before = before + jnp.sum(mine, axis=1, keepdims=True)
        value = total[v : v + 1] * gain[v] * scale * mine
        for k in range(3):
            outs[k] = outs[k] + jnp.sum(jnp.where(slot == float(k), value, 0.0), axis=1, keepdims=True)
    for k in range(3):
        energy_ref[:, k : k + 1] = outs[k]

    for one in (xa1, xb1, xa0, xb0, ya1, yb1, ya0, yb0, ea, fa):
        left_for_good(*one)


def shards(state, sigma, vert, bal_temp, chi_coef, scales, classes, owner):
    dims = (lax.axis_size("lat"), lax.axis_size("lon"), state.shape[1], sigma.shape[2])
    spec, scratch = layout(*dims, scales.shape[0])
    vmem = pl.BlockSpec(memory_space=pltpu.VMEM)
    return pl.pallas_call(
        functools.partial(kernel, dims, spec, tuple(scratch)),
        out_shape=(pltpu.VMEM(state.shape, F32), pltpu.VMEM((1, 3), F32)),
        in_specs=[pl.BlockSpec(memory_space=pltpu.MemorySpace.HBM)] * 8,
        out_specs=(vmem, vmem),
        scratch_shapes=list(scratch.values()),
        compiler_params=pltpu.CompilerParams(
            collective_id=0, has_side_effects=True, vmem_limit_bytes=56 * 1024 * 1024
        ),
        name="covariance",
    )(
        state,
        sigma,
        vert,
        bal_temp,
        chi_coef.reshape(1, -1),
        scales.reshape(1, -1),
        classes.reshape(1, -1),
        owner.reshape(1, -1),
    )


def solution(mesh):
    return jax.shard_map(
        shards,
        mesh=mesh,
        in_specs=(P(None, "lat", "lon"), P(None, "lat", "lon"), P(), P(), P(), P(), P(), P()),
        out_specs=(P(None, "lat", "lon"), P(("lat", "lon"), None)),
        check_vma=False,
    )
```

time: 383 us -> 46.3 us (0.12)
  the two profiles are of different devices: /device:TPU:3 before, /device:TPU:1 now
where the time goes in v2:
time: 46.3 us; the launch traced here: 46.2 us
  Pallas kernels  43.8 us (95%)
  local copies, waits for them, and re-layouts  1.72 us (4%)
  between operations  0.64 us (1%)
    pallas_call x1, Pallas kernels, shards(): pl.pallas_call(functools.partial(kernel, dims, spec, tuple(scratch)), out...  43.8 us
    unnamed x2, local copies, waits for them, and re-layouts  1.72 us

profile of v2, /device:TPU:1, one launch (start us, length us, event | category | flops | bytes accessed | tf_op | source)
XLA Modules:
  0.0 46.2 jit_solution(8818673097073339659)
XLA Ops:
  0.6 43.8 %covariance.1 = (f32[3,24,6144]{2,1,0:T(8,128)S(1)}, f32[1,3]{1,0:T(1,128)S(1)}) custom-call(f32[3,24,6144]{2,1,0:T(8,128)} %state_hbm.1, f32[3,24,96]{2,1,0:T(8,128)} %sigma_hbm.1, f32[3,64,64]{2,1,0:T(8,128)} %vert_hbm.1, f32[64,64]{1,0:T(8,128)} %bal_hbm.1, f32[1,64]{1,0:T(1,128)} %bitcast.6, f32[1,8]{1,0:T(1,128)} %bitcast.7, s32[1,192]{1,0:T(1,128)} %bitcast.4, ...), custom_call_target="tpu_custom_call" | custom-call | tf_op jit(solution)/shard_map/covariance/pallas_call | solution.py:828
  44.5 1.2 %copy.12 = f32[3,24,6144]{2,1,0:T(8,128)} copy(f32[3,24,6144]{2,1,0:T(8,128)S(1)} %get-tuple-element.2) | data formatting | bytes 3538944
  45.7 0.5 %copy.13 = f32[1,3]{1,0:T(1,128)} copy(f32[1,3]{1,0:T(1,128)S(1)} %get-tuple-element.3) | data formatting | bytes 24

commit v3 on v2

--- a/solution.py
+++ b/solution.py
@@ -35,7 +35,7 @@
     for c, count in enumerate((1, 2)):
         spec[f"x_rows{c}"] = -(-count * groups * 2 // 8) * 8
         spec[f"y_rows{c}"] = -(-(count * jj_n * 4 + (4 if c == 0 else 0)) // 8) * 8
-        spec[f"y_stride{c}"] = count * half + (8 if c == 0 else 0)
+        spec[f"y_stride{c}"] = count * half + 8
     shapes = {
         "in_sem": 3,
         "small_sem": 7,
@@ -82,8 +82,11 @@
         for name in ("send", "recv", "back", "home"):
             sizes[f"x_{name}{c}"] = n_lon * spec[f"x_rows{c}"]
             sizes[f"y_{name}{c}"] = n_lat * spec[f"y_rows{c}"]
+        for name in ("send", "recv"):
+            sizes[f"z_{name}{c}"] = n_lat * spec[f"y_rows{c}"]
         for name in ("ss", "rs", "bss", "brs"):
             shapes[f"x_{name}{c}"] = pltpu.SemaphoreType.DMA((1,))
+            shapes[f"z_{name}{c}"] = pltpu.SemaphoreType.DMA((1,))
             shapes[f"y_{name}{c}"] = pltpu.SemaphoreType.DMA((1,))
     for name, size in sizes.items():
         shapes[name] = vm(size)
@@ -374,10 +377,10 @@
     def part(ref, slot, size):
         return ref.at[pl.ds(pl.multiple_of(slot * size, 8), size)]
 
-    def way(axis, c, back):
+    def way(axis, c, back, k=None):
         me, n = (la, n_lat) if axis == "lat" else (lo, n_lon)
-        k = "y" if axis == "lat" else "x"
-        size = spec[f"{k}_rows{c}"]
+        k = k or ("y" if axis == "lat" else "x")
+        size = spec[f"{k.replace('z', 'y')}_rows{c}"]
         a, b, ss, rs = ("back", "home", "bss", "brs") if back else ("send", "recv", "ss", "rs")
         return axis, me, n, size, *(R.at(f"{k}_{name}", c) for name in (a, b, ss, rs))
 
@@ -516,17 +519,60 @@
         send, size = R.at("y_send", c), spec[f"y_rows{c}"]
         for k, states in enumerate((s1, t1, s2, t2)):
             for i in range(len(vs)):
-                for q in range(jj_n):
-                    send[pl.ds((i * jj_n + q) * 4 + k, n_lat, stride=size), :] = states[i][
-                        q * n_lat : (q + 1) * n_lat
-                    ]
+                put_states(send, size, i, k, states[i])
             if c == 0:
                 last = jj_n * 4 + k
                 send[pl.ds(last, n_lat, stride=size), :] = jnp.zeros((n_lat, 128), F32)
                 send[pl.ds(last, 1), :] = states[0][half : half + 1]
         return s2, t2
 
-    def y_scan(c):
+    def w_row(v, i):
+        every = rows if v == 0 else 2 * rows
+        return w_ref(v)[pl.ds((0 if v == 0 else (v - 1) * rows) + i, half, stride=every), :]
+
+    def put_states(send, size, i, k, value):
+        for q in range(jj_n):
+            send[pl.ds((i * jj_n + q) * 4 + k, n_lat, stride=size), :] = value[q * n_lat : (q + 1) * n_lat]
+
+    def w_states(c):
+        send, size, stride = R.at("z_send", c), spec[f"y_rows{c}"], spec[f"y_stride{c}"]
+        if c == 0:
+            send[...] = jnp.zeros_like(send)
+        for i, v in enumerate(CHUNKS[c]):
+            base = y_parts(c)[i][0]
+
+            def at(n):
+                return pl.ds(pl.multiple_of(n * stride + base, 8), half)
+
+            def put(name):
+                def go(n, value):
+                    R.at(name, c)[at(n), :] = value[0]
+
+                return go
+
+            zero = (jnp.zeros((half, 128), F32),)
+            times = lambda s: [decay[v] * s[0]]
+            (s1,), (t1,) = both_ways(rows, lambda n: [w_row(v, n)], put("ys"), put("yt"), times, zero)
+            second = lambda n: [R.at("ys", c)[at(n), :] + R.at("yt", c)[at(n), :]]
+            skip = lambda n, value: None
+            (s2,), (t2,) = both_ways(rows, second, skip, skip, times, zero)
+            for k, value in enumerate((s1, t1, s2, t2)):
+                put_states(send, size, i, k, value)
+
+    def local_energy(c):
+        stride, out = spec[f"y_stride{c}"], []
+        for i, v in enumerate(CHUNKS[c]):
+            base = y_parts(c)[i][0]
+
+            def step(n, acc):
+                at = pl.ds(pl.multiple_of(n * stride + base, 8), half)
+                return acc + w_row(v, n) * (R.at("yu", c)[at, :] + R.at("yv", c)[at, :])
+
+            acc = lax.fori_loop(0, rows, step, jnp.zeros((half, 128), F32), unroll=4)
+            out.append(jnp.sum(acc, axis=0, keepdims=True))
+        return out
+
+    def y_scan(c, energy):
         vs = CHUNKS[c]
         count, size = len(vs) * jj_n + (1 if c == 0 else 0), spec[f"y_rows{c}"]
         jumps = jj_n if c else count
@@ -553,6 +599,15 @@
         )
         give(2, s_in2)
         give(3, t_in2)
+        w_in = R.at("z_recv", c)
+        far = jnp.zeros((count, 128), F32)
+        for e in range(n_lat):
+            p = [w_in[pl.ds(e * size + k, count, stride=4), :] for k in range(4)]
+            far = far + s_in2[e] * p[1] + t_in2[e] * p[0] + s_in[e] * p[3] + t_in[e] * p[2]
+        far = a_r * far
+        for i, v in enumerate(vs):
+            own = jnp.sum(far[i * jj_n : (i + 1) * jj_n], axis=0, keepdims=True)
+            R.e_send[pl.ds(v, 1), :] = energy[i] + own
 
     def y_finish(c, s2, t2):
         home, size = R.at("y_home", c), spec[f"y_rows{c}"]
@@ -591,15 +646,10 @@
     def mix_out(c):
         yf, stride = R.at("yf", c), spec[f"y_stride{c}"]
 
-        def step(b, acc):
+        def step(b, _):
             js = batch(b)
-            acc = list(acc)
             for i, v in enumerate(CHUNKS[c]):
-                parts = []
-                for j in js:
-                    x = yf[pl.ds(i * half + j, rows, stride=stride), :]
-                    acc[i] = acc[i] + x * block(w_ref(v), w_at(v, j))
-                    parts.append(x)
+                parts = [yf[pl.ds(i * half + j, rows, stride=stride), :] for j in js]
                 y = split_product(rows_of(parts), mats[3 + v])
                 tile = sig[pl.ds(v * rows, rows), :]
                 for t, j in enumerate(js):
@@ -608,12 +658,9 @@
                         put_block(temp, (j + 1) * rows, z)
                     else:
                         put_block(R.w1, w_at(v, j), z)
-            return tuple(acc)
-
-        start = tuple(jnp.zeros((rows, 128), F32) for _ in CHUNKS[c])
-        acc = lax.fori_loop(0, half // 8, step, start, unroll=True)
-        for i, v in enumerate(CHUNKS[c]):
-            R.e_send[pl.ds(v, 1), :] = jnp.sum(acc[i], axis=0, keepdims=True)
+            return 0
+
+        lax.fori_loop(0, half // 8, step, 0, unroll=True)
 
     kept = {1: x_filter(1)}
     pl.semaphore_wait(barrier, n_lat + n_lon - 2)
@@ -639,6 +686,7 @@
         halo.append(copy)
     xa1, xb1, xa0, xb0 = way("lon", 1, False), way("lon", 1, True), way("lon", 0, False), way("lon", 0, True)
     ya1, yb1, ya0, yb0 = way("lat", 1, False), way("lat", 1, True), way("lat", 0, False), way("lat", 0, True)
+    za1, za0 = way("lat", 1, False, "z"), way("lat", 0, False, "z")
     exchange(*xa1)
 
     loads[0].wait()
@@ -688,6 +736,9 @@
 
     own_up, own_down = row_sigma(sig0, 0), row_sigma(sig0, rows - 1)
     own_side = side_sigma(sig0, 0, sig0, cols - 1)
+
+    w_states(1)
+    exchange(*za1)
 
     arrive(*xa1)
     x_scan(1)
@@ -720,6 +771,8 @@
 
     kept[0] = x_filter(0)
     exchange(*xa0)
+    w_states(0)
+    exchange(*za0)
 
     arrive(*xb1)
     arrive(*xa0)
@@ -742,23 +795,36 @@
         0,
     )
 
+    R.e_send[...] = jnp.zeros_like(R.e_send)
+    near1, near0 = local_energy(1), local_energy(0)
+
+    arrive(*za1)
     arrive(*ya1)
-    y_scan(1)
+    y_scan(1, near1)
     exchange(*yb1)
+    arrive(*za0)
     arrive(*ya0)
-    y_scan(0)
+    y_scan(0, near0)
     exchange(*yb0)
-
-    R.e_send[...] = jnp.zeros_like(R.e_send)
+    ea = ("lat", la, n_lat, 8, R.e_send, R.e_recv, R.e_ss, R.e_rs)
+    exchange(*ea, shared=True)
+
+    def total_of(ref, n):
+        total = ref[pl.ds(0, 8), :]
+        for e in range(1, n):
+            total = total + ref[pl.ds(e * 8, 8), :]
+        return total
+
     arrive(*yb1)
     y_finish(1, *ends1)
     mix_out(1)
+    arrive(*ea, shared=True)
+    R.f_send[...] = total_of(R.e_recv, n_lat)
+    fa = ("lon", lo, n_lon, 8, R.f_send, R.f_recv, R.f_ss, R.f_rs)
+    exchange(*fa, shared=True)
     arrive(*yb0)
     y_finish(0, *ends0)
     mix_out(0)
-    ea = ("lat", la, n_lat, 8, R.e_send, R.e_recv, R.e_ss, R.e_rs)
-    exchange(*ea, shared=True)
-
     edges = split_product(
         rows_of([edge_rows[...], R.yf0[pl.ds(half, rows, stride=spec["y_stride0"]), :]]), mats[3]
     )
@@ -785,16 +851,6 @@
 
     lax.fori_loop(0, half // 8, finish, 0, unroll=True)
 
-    def total_of(ref, n):
-        total = ref[pl.ds(0, 8), :]
-        for e in range(1, n):
-            total = total + ref[pl.ds(e * 8, 8), :]
-        return total
-
-    arrive(*ea, shared=True)
-    R.f_send[...] = total_of(R.e_recv, n_lat)
-    fa = ("lon", lo, n_lon, 8, R.f_send, R.f_recv, R.f_ss, R.f_rs)
-    exchange(*fa, shared=True)
     arrive(*fa, shared=True)
     total = total_of(R.f_recv, n_lon)
     total = total + swap(total)
@@ -817,7 +873,7 @@
     for k in range(3):
         energy_ref[:, k : k + 1] = outs[k]
 
-    for one in (xa1, xb1, xa0, xb0, ya1, yb1, ya0, yb0, ea, fa):
+    for one in (xa1, xb1, xa0, xb0, za1, za0, ya1, yb1, ya0, yb0, ea, fa):
         left_for_good(*one)
 
 

time: 46.3 us -> 41.5 us (0.90)
  Pallas kernels: 43.8 us -> 39 us
    pallas_call x1, Pallas kernels: 43.8 us -> 39 us  [shards(): pl.pallas_call(functools.partial(kernel, dims, spec, tuple(scratch)), out...]
where the time goes in v3:
time: 41.5 us; the launch traced here: 41.4 us
  Pallas kernels  39 us (94%)
  local copies, waits for them, and re-layouts  1.72 us (4%)
  between operations  0.64 us (2%)
    pallas_call x1, Pallas kernels, shards(): pl.pallas_call(functools.partial(kernel, dims, spec, tuple(scratch)), out...  39 us
    unnamed x2, local copies, waits for them, and re-layouts  1.72 us

profile of v3, /device:TPU:1, one launch (start us, length us, event | category | flops | bytes accessed | tf_op | source)
XLA Modules:
  0.0 41.4 jit_solution(5181998806750308427)
XLA Ops:
  0.6 39.0 %covariance.1 = (f32[3,24,6144]{2,1,0:T(8,128)S(1)}, f32[1,3]{1,0:T(1,128)S(1)}) custom-call(f32[3,24,6144]{2,1,0:T(8,128)} %state_hbm.1, f32[3,24,96]{2,1,0:T(8,128)} %sigma_hbm.1, f32[3,64,64]{2,1,0:T(8,128)} %vert_hbm.1, f32[64,64]{1,0:T(8,128)} %bal_hbm.1, f32[1,64]{1,0:T(1,128)} %bitcast.6, f32[1,8]{1,0:T(1,128)} %bitcast.7, s32[1,192]{1,0:T(1,128)} %bitcast.4, ...), custom_call_target="tpu_custom_call" | custom-call | tf_op jit(solution)/shard_map/covariance/pallas_call | solution.py:884
  39.7 1.2 %copy.12 = f32[3,24,6144]{2,1,0:T(8,128)} copy(f32[3,24,6144]{2,1,0:T(8,128)S(1)} %get-tuple-element.2) | data formatting | bytes 3538944
  40.9 0.5 %copy.13 = f32[1,3]{1,0:T(1,128)} copy(f32[1,3]{1,0:T(1,128)S(1)} %get-tuple-element.3) | data formatting | bytes 24

commit v4 on v3

--- a/solution.py
+++ b/solution.py
@@ -33,7 +33,7 @@
     groups = rows // 8
     spec = {}
     for c, count in enumerate((1, 2)):
-        spec[f"x_rows{c}"] = -(-count * groups * 2 // 8) * 8
+        spec[f"x_rows{c}"] = -(-count * groups * 2 // 8) * 8 if c else 2 * rows
         spec[f"y_rows{c}"] = -(-(count * jj_n * 4 + (4 if c == 0 else 0)) // 8) * 8
         spec[f"y_stride{c}"] = count * half + 8
     shapes = {
@@ -81,6 +81,8 @@
             sizes[f"{name}{c}"] = rows * spec[f"y_stride{c}"]
         for name in ("send", "recv", "back", "home"):
             sizes[f"x_{name}{c}"] = n_lon * spec[f"x_rows{c}"]
+            if c == 0 and name == "send":
+                sizes[f"x_{name}{c}"] = spec[f"x_rows{c}"]
             sizes[f"y_{name}{c}"] = n_lat * spec[f"y_rows{c}"]
         for name in ("send", "recv"):
             sizes[f"z_{name}{c}"] = n_lat * spec[f"y_rows{c}"]
@@ -94,6 +96,12 @@
 
 
 CHUNKS = ((0,), (1, 2))
+
+
+def far_first(n, step):
+    ring = lambda d, size: min(d, size - d)
+    hops = lambda o: ring(o // step, n // step) + (ring(o % step, step) if step > 2 else 0)
+    return sorted(range(1, n), key=lambda o: (-hops(o), o))
 
 
 class Names:
@@ -133,9 +141,10 @@
     lo = lax.axis_index("lon")
 
     barrier = pltpu.get_barrier_semaphore()
-    for o in range(1, n_lat):
+    lat_order, lon_order = far_first(n_lat, 4), far_first(n_lon, 2)
+    for o in lat_order:
         pl.semaphore_signal(barrier, inc=1, device_id=(lax.rem(la + o, n_lat), lo), device_id_type=MESH)
-    for o in range(1, n_lon):
+    for o in lon_order:
         pl.semaphore_signal(barrier, inc=1, device_id=(la, lax.rem(lo + o, n_lon)), device_id_type=MESH)
 
     sigma_ref, vert_ref, bal_ref = R.sigma, R.vert, R.bal
@@ -359,6 +368,9 @@
         q1 = pick(t1 + ah * t1r, t2r + g1 * t1 + ah * (t2 + g2 * s1r))
         send = R.at("x_send", c)
         for i, q in enumerate((q0, q1)):
+            if c == 0:
+                send[pl.ds(i * rows, rows), :] = q
+                continue
             for g in range(full // 8):
                 send[pl.ds(g * 2 + i, 8, stride=spec[f"x_rows{c}"]), :] = q[g * 8 : g * 8 + 8]
         return dict(s1r=s1r, t1r=t1r, s2=s2, t2=t2, ah=ah, g1=g1, g2=g2, ax=ax)
@@ -385,7 +397,7 @@
         return axis, me, n, size, *(R.at(f"{k}_{name}", c) for name in (a, b, ss, rs))
 
     def exchange(axis, me, n, size, src, dst, ss, rs, shared=False):
-        for o in range(1, n):
+        for o in lat_order if axis == "lat" else lon_order:
             other = lax.rem(me + o, n)
             remote(axis, other, src if shared else part(src, other, size), part(dst, me, size), ss, rs).start()
         pltpu.make_async_copy(src if shared else part(src, me, size), part(dst, me, size), rs.at[0]).start()
@@ -427,10 +439,14 @@
     def x_scan(c):
         vs = CHUNKS[c]
         count, size = len(vs) * groups, spec[f"x_rows{c}"]
+        if c == 0:
+            count = rows
+            spots = [[pl.ds(e * size + i * rows, rows) for e in range(n_lon)] for i in (0, 1)]
+        else:
+            spots = [[pl.ds(e * size + i, count, stride=2) for e in range(n_lon)] for i in (0, 1)]
         a_r, an_r, g1_r, g2_r = scan_coefs(vs, count, groups, cols)
         recv, back = R.at("x_recv", c), R.at("x_back", c)
-        p0 = [recv[pl.ds(e * size, count, stride=2), :] for e in range(n_lon)]
-        p1 = [recv[pl.ds(e * size + 1, count, stride=2), :] for e in range(n_lon)]
+        p0, p1 = ([recv[at, :] for at in line] for line in spots)
         s_in, t_in = scan_states(n_lon, p0, p1, an_r, a_r)
         sr = [swap(x) for x in s_in]
         tr = [swap(x) for x in t_in]
@@ -442,17 +458,20 @@
             a_r,
         )
         for e in range(n_lon):
-            back[pl.ds(e * size, count, stride=2), :] = pick(s_in[e], s_in2[e])
-            back[pl.ds(e * size + 1, count, stride=2), :] = pick(t_in[e], t_in2[e])
+            back[spots[0][e], :] = pick(s_in[e], s_in2[e])
+            back[spots[1][e], :] = pick(t_in[e], t_in2[e])
 
     def x_finish(c, k):
         vs = CHUNKS[c]
         full = len(vs) * rows
         stride = spec[f"y_stride{c}"]
-        home, yf, xe = R.at("x_home", c), R.at("yf", c), R.at("xe", c)
+        yf, xe = R.at("yf", c), R.at("xe", c)
         xt, xv = R.at("xu", c), R.at("xv", c)
 
         def got(i):
+            if c == 0:
+                return block(R.x_back0, lo * spec["x_rows0"] + i * rows)
+            home = R.x_home1
             return rows_of(
                 [home[pl.ds(g * 2 + i, 8, stride=spec[f"x_rows{c}"]), :] for g in range(full // 8)]
             )
@@ -684,7 +703,7 @@
         )
         copy.start()
         halo.append(copy)
-    xa1, xb1, xa0, xb0 = way("lon", 1, False), way("lon", 1, True), way("lon", 0, False), way("lon", 0, True)
+    xa1, xb1, xa0 = way("lon", 1, False), way("lon", 1, True), way("lon", 0, False)
     ya1, yb1, ya0, yb0 = way("lat", 1, False), way("lat", 1, True), way("lat", 0, False), way("lat", 0, True)
     za1, za0 = way("lat", 1, False, "z"), way("lat", 0, False, "z")
     exchange(*xa1)
@@ -736,9 +755,6 @@
 
     own_up, own_down = row_sigma(sig0, 0), row_sigma(sig0, rows - 1)
     own_side = side_sigma(sig0, 0, sig0, cols - 1)
-
-    w_states(1)
-    exchange(*za1)
 
     arrive(*xa1)
     x_scan(1)
@@ -770,18 +786,18 @@
     R.w0[at_last, :] = R.w0[at_last, :] - pick(zero_block, side)
 
     kept[0] = x_filter(0)
-    exchange(*xa0)
+    exchange(*xa0, shared=True)
+    w_states(1)
+    exchange(*za1)
     w_states(0)
     exchange(*za0)
 
     arrive(*xb1)
-    arrive(*xa0)
-    x_scan(0)
-    exchange(*xb0)
     x_finish(1, kept[1])
     ends1 = y_filter(1)
     exchange(*ya1)
-    arrive(*xb0)
+    arrive(*xa0, shared=True)
+    x_scan(0)
     x_finish(0, kept[0])
     ends0 = y_filter(0)
     exchange(*ya0)
@@ -805,9 +821,9 @@
     arrive(*za0)
     arrive(*ya0)
     y_scan(0, near0)
-    exchange(*yb0)
     ea = ("lat", la, n_lat, 8, R.e_send, R.e_recv, R.e_ss, R.e_rs)
     exchange(*ea, shared=True)
+    exchange(*yb0)
 
     def total_of(ref, n):
         total = ref[pl.ds(0, 8), :]
@@ -815,13 +831,13 @@
             total = total + ref[pl.ds(e * 8, 8), :]
         return total
 
-    arrive(*yb1)
-    y_finish(1, *ends1)
-    mix_out(1)
     arrive(*ea, shared=True)
     R.f_send[...] = total_of(R.e_recv, n_lat)
     fa = ("lon", lo, n_lon, 8, R.f_send, R.f_recv, R.f_ss, R.f_rs)
     exchange(*fa, shared=True)
+    arrive(*yb1)
+    y_finish(1, *ends1)
+    mix_out(1)
     arrive(*yb0)
     y_finish(0, *ends0)
     mix_out(0)
@@ -873,7 +889,7 @@
     for k in range(3):
         energy_ref[:, k : k + 1] = outs[k]
 
-    for one in (xa1, xb1, xa0, xb0, za1, za0, ya1, yb1, ya0, yb0, ea, fa):
+    for one in (xa1, xb1, xa0, za1, za0, ya1, yb1, ya0, yb0, ea, fa):
         left_for_good(*one)
 
 

time: 41.5 us -> 38.2 us (0.920)
  Pallas kernels: 39 us -> 35.7 us
    pallas_call x1, Pallas kernels: 39 us -> 35.7 us  [shards(): pl.pallas_call(functools.partial(kernel, dims, spec, tuple(scratch)), out...]
where the time goes in v4:
time: 38.2 us; the launch traced here: 38 us
  Pallas kernels  35.7 us (93%)
  local copies, waits for them, and re-layouts  1.72 us (5%)
  between operations  0.64 us (2%)
    pallas_call x1, Pallas kernels, shards(): pl.pallas_call(functools.partial(kernel, dims, spec, tuple(scratch)), out...  35.7 us
    unnamed x2, local copies, waits for them, and re-layouts  1.72 us

profile of v4, /device:TPU:1, one launch (start us, length us, event | category | flops | bytes accessed | tf_op | source)
XLA Modules:
  0.0 38.0 jit_solution(3609541992132092423)
XLA Ops:
  0.6 35.7 %covariance.1 = (f32[3,24,6144]{2,1,0:T(8,128)S(1)}, f32[1,3]{1,0:T(1,128)S(1)}) custom-call(f32[3,24,6144]{2,1,0:T(8,128)} %state_hbm.1, f32[3,24,96]{2,1,0:T(8,128)} %sigma_hbm.1, f32[3,64,64]{2,1,0:T(8,128)} %vert_hbm.1, f32[64,64]{1,0:T(8,128)} %bal_hbm.1, f32[1,64]{1,0:T(1,128)} %bitcast.6, f32[1,8]{1,0:T(1,128)} %bitcast.7, s32[1,192]{1,0:T(1,128)} %bitcast.4, ...), custom_call_target="tpu_custom_call" | custom-call | tf_op jit(solution)/shard_map/covariance/pallas_call | solution.py:900
  36.3 1.2 %copy.12 = f32[3,24,6144]{2,1,0:T(8,128)} copy(f32[3,24,6144]{2,1,0:T(8,128)S(1)} %get-tuple-element.2) | data formatting | bytes 3538944
  37.5 0.5 %copy.13 = f32[1,3]{1,0:T(1,128)} copy(f32[1,3]{1,0:T(1,128)S(1)} %get-tuple-element.3) | data formatting | bytes 24

commit v5 on v4

--- a/solution.py
+++ b/solution.py
@@ -817,12 +817,12 @@
     arrive(*za1)
     arrive(*ya1)
     y_scan(1, near1)
-    exchange(*yb1)
     arrive(*za0)
     arrive(*ya0)
     y_scan(0, near0)
     ea = ("lat", la, n_lat, 8, R.e_send, R.e_recv, R.e_ss, R.e_rs)
     exchange(*ea, shared=True)
+    exchange(*yb1)
     exchange(*yb0)
 
     def total_of(ref, n):
@@ -867,27 +867,28 @@
 
     lax.fori_loop(0, half // 8, finish, 0, unroll=True)
 
-    arrive(*fa, shared=True)
-    total = total_of(R.f_recv, n_lon)
-    total = total + swap(total)
-
     rank = (la * n_lon + lo).astype(F32)
-    keep = lane[:1] < 64
     strict = (
         lax.broadcasted_iota(jnp.int32, (128, 128), 0) < lax.broadcasted_iota(jnp.int32, (128, 128), 1)
     ).astype(F32)
     before = jnp.zeros((1, 1), F32)
-    outs = [jnp.zeros((1, 1), F32)] * 3
+    weights = [[], [], []]
     scale = 1.0 / float(rows * n_lat * cols * n_lon)
     for v in range(3):
-        mine = jnp.where(keep & (owners[v] == rank), 1.0, 0.0)
+        mine = jnp.where(low1 & (owners[v] == rank), 1.0, 0.0)
         slot = jnp.dot(jnp.broadcast_to(mine, (8, 128)), strict, preferred_element_type=F32)[:1] + before
         before = before + jnp.sum(mine, axis=1, keepdims=True)
-        value = total[v : v + 1] * gain[v] * scale * mine
         for k in range(3):
-            outs[k] = outs[k] + jnp.sum(jnp.where(slot == float(k), value, 0.0), axis=1, keepdims=True)
+            weights[k].append(jnp.where(slot == float(k), gain[v] * scale * mine, 0.0))
+    zeros = jnp.zeros((5, 128), F32)
+    weights = [rows_of(line + [zeros]) for line in weights]
+
+    arrive(*fa, shared=True)
+    total = total_of(R.f_recv, n_lon)
+    total = total + swap(total)
     for k in range(3):
-        energy_ref[:, k : k + 1] = outs[k]
+        share = jnp.sum(total * weights[k], axis=0, keepdims=True)
+        energy_ref[:, k : k + 1] = jnp.sum(share, axis=1, keepdims=True)
 
     for one in (xa1, xb1, xa0, za1, za0, ya1, yb1, ya0, yb0, ea, fa):
         left_for_good(*one)

time: 38.2 us -> 37.8 us (0.990)
  Pallas kernels: 35.7 us -> 35.3 us
where the time goes in v5:
time: 37.8 us; the launch traced here: 37.7 us
  Pallas kernels  35.3 us (93%)
  local copies, waits for them, and re-layouts  1.72 us (5%)
  between operations  0.64 us (2%)
    pallas_call x1, Pallas kernels, shards(): pl.pallas_call(functools.partial(kernel, dims, spec, tuple(scratch)), out...  35.3 us
    unnamed x2, local copies, waits for them, and re-layouts  1.72 us

profile of v5, /device:TPU:1, one launch (start us, length us, event | category | flops | bytes accessed | tf_op | source)
XLA Modules:
  0.0 37.7 jit_solution(5005678030475303281)
XLA Ops:
  0.6 35.3 %covariance.1 = (f32[3,24,6144]{2,1,0:T(8,128)S(1)}, f32[1,3]{1,0:T(1,128)S(1)}) custom-call(f32[3,24,6144]{2,1,0:T(8,128)} %state_hbm.1, f32[3,24,96]{2,1,0:T(8,128)} %sigma_hbm.1, f32[3,64,64]{2,1,0:T(8,128)} %vert_hbm.1, f32[64,64]{1,0:T(8,128)} %bal_hbm.1, f32[1,64]{1,0:T(1,128)} %bitcast.6, f32[1,8]{1,0:T(1,128)} %bitcast.7, s32[1,192]{1,0:T(1,128)} %bitcast.4, ...), custom_call_target="tpu_custom_call" | custom-call | tf_op jit(solution)/shard_map/covariance/pallas_call | solution.py:901
  35.9 1.2 %copy.12 = f32[3,24,6144]{2,1,0:T(8,128)} copy(f32[3,24,6144]{2,1,0:T(8,128)S(1)} %get-tuple-element.2) | data formatting | bytes 3538944
  37.2 0.5 %copy.13 = f32[1,3]{1,0:T(1,128)} copy(f32[1,3]{1,0:T(1,128)S(1)} %get-tuple-element.3) | data formatting | bytes 24

commit v6 on v5

--- a/solution.py
+++ b/solution.py
@@ -69,9 +69,9 @@
         "halo_send": 2 * (half + rows) + 4 * rows,
         "halo_recv": 2 * (half + rows) + 4 * rows,
         "e_send": 8,
-        "e_recv": 8 * n_lat,
+        "e_recv": 8 * n_lon,
         "f_send": 8,
-        "f_recv": 8 * n_lon,
+        "f_recv": 8 * n_lat,
     }
     for c, count in enumerate((1, 2)):
         for name in ("w", "xs", "xt", "xu", "xv"):
@@ -820,7 +820,7 @@
     arrive(*za0)
     arrive(*ya0)
     y_scan(0, near0)
-    ea = ("lat", la, n_lat, 8, R.e_send, R.e_recv, R.e_ss, R.e_rs)
+    ea = ("lon", lo, n_lon, 8, R.e_send, R.e_recv, R.e_ss, R.e_rs)
     exchange(*ea, shared=True)
     exchange(*yb1)
     exchange(*yb0)
@@ -832,8 +832,8 @@
         return total
 
     arrive(*ea, shared=True)
-    R.f_send[...] = total_of(R.e_recv, n_lat)
-    fa = ("lon", lo, n_lon, 8, R.f_send, R.f_recv, R.f_ss, R.f_rs)
+    R.f_send[...] = total_of(R.e_recv, n_lon)
+    fa = ("lat", la, n_lat, 8, R.f_send, R.f_recv, R.f_ss, R.f_rs)
     exchange(*fa, shared=True)
     arrive(*yb1)
     y_finish(1, *ends1)
@@ -884,7 +884,7 @@
     weights = [rows_of(line + [zeros]) for line in weights]
 
     arrive(*fa, shared=True)
-    total = total_of(R.f_recv, n_lon)
+    total = total_of(R.f_recv, n_lat)
     total = total + swap(total)
     for k in range(3):
         share = jnp.sum(total * weights[k], axis=0, keepdims=True)

time: 37.8 us -> 36.8 us (0.974)
  Pallas kernels: 35.3 us -> 34.3 us
    pallas_call x1, Pallas kernels: 35.3 us -> 34.3 us  [shards(): pl.pallas_call(functools.partial(kernel, dims, spec, tuple(scratch)), out...]
where the time goes in v6:
time: 36.8 us; the launch traced here: 36.7 us
  Pallas kernels  34.3 us (93%)
  local copies, waits for them, and re-layouts  1.72 us (5%)
  between operations  0.64 us (2%)
    pallas_call x1, Pallas kernels, shards(): pl.pallas_call(functools.partial(kernel, dims, spec, tuple(scratch)), out...  34.3 us
    unnamed x2, local copies, waits for them, and re-layouts  1.72 us

profile of v6, /device:TPU:1, one launch (start us, length us, event | category | flops | bytes accessed | tf_op | source)
XLA Modules:
  0.0 36.7 jit_solution(1854675379072184212)
XLA Ops:
  0.6 34.3 %covariance.1 = (f32[3,24,6144]{2,1,0:T(8,128)S(1)}, f32[1,3]{1,0:T(1,128)S(1)}) custom-call(f32[3,24,6144]{2,1,0:T(8,128)} %state_hbm.1, f32[3,24,96]{2,1,0:T(8,128)} %sigma_hbm.1, f32[3,64,64]{2,1,0:T(8,128)} %vert_hbm.1, f32[64,64]{1,0:T(8,128)} %bal_hbm.1, f32[1,64]{1,0:T(1,128)} %bitcast.6, f32[1,8]{1,0:T(1,128)} %bitcast.7, s32[1,192]{1,0:T(1,128)} %bitcast.4, ...), custom_call_target="tpu_custom_call" | custom-call | tf_op jit(solution)/shard_map/covariance/pallas_call | solution.py:901
  35.0 1.2 %copy.12 = f32[3,24,6144]{2,1,0:T(8,128)} copy(f32[3,24,6144]{2,1,0:T(8,128)S(1)} %get-tuple-element.2) | data formatting | bytes 3538944
  36.2 0.5 %copy.13 = f32[1,3]{1,0:T(1,128)} copy(f32[1,3]{1,0:T(1,128)S(1)} %get-tuple-element.3) | data formatting | bytes 24
